TPU v7x, 32 devices: a whole 2x2x4 slice. The times are simulated.
32 devices in a mesh: dp: 4 (over z), seq: 8 (over y, x, core).
Axes of the slice: x: 2, y: 2, z: 4, core: 2. Of those that a mesh axis runs over, the one named last changes fastest.
Arguments:
- view_fine: bfloat16 [4, 768, 768], P('dp', 'seq'), may hold values from -6 to 6
- view_mid: bfloat16 [4, 384, 768], P('dp', 'seq'), may hold values from -6 to 6
- view_coarse: bfloat16 [4, 192, 768], P('dp', 'seq'), may hold values from -6 to 6
- grad_fine: bfloat16 [4, 768, 768], P('dp', 'seq'), may hold values from -6 to 6
- grad_mid: bfloat16 [4, 384, 768], P('dp', 'seq'), may hold values from -6 to 6
- grad_coarse: bfloat16 [4, 192, 768], P('dp', 'seq'), may hold values from -6 to 6
- clip_ids: int32 [4, 192], P('dp'), may hold values from 0 to 3, never falling along the last dimension, each value on 1 to 144 neighbouring positions
- attn_in: bfloat16 [6912, 768], P(('dp', 'seq')), may hold values from -0.21875 to 0.21875
- attn_out: bfloat16 [2304, 768], P(('dp', 'seq')), may hold values from -1.75 to 1.75
- mlp_w: bfloat16 [4608, 3072], P(('dp', 'seq')), may hold values from -0.21875 to 0.21875
- cross_in: bfloat16 [4608, 768], P(('dp', 'seq')), may hold values from -0.21875 to 0.21875
- cross_out: bfloat16 [1536, 768], P(('dp', 'seq')), may hold values from -1.75 to 1.75
- norm_gains: bfloat16 [10, 768], P(None, ('dp', 'seq')), may hold values from 0.5 to 1.5
- biases: bfloat16 [28, 768], P(None, ('dp', 'seq')), may hold values from -0.59765625 to 0.59765625
- ffn_bias: bfloat16 [3, 3072], P(None, ('dp', 'seq')), may hold values from -2 to 2
Outputs:
- out_fine: bfloat16 [4, 768, 768], P('dp', 'seq')
- out_mid: bfloat16 [4, 384, 768], P('dp', 'seq')
- out_coarse: bfloat16 [4, 192, 768], P('dp', 'seq')
- dx_fine: float32 [4, 768, 768], P('dp', 'seq')
- dx_mid: float32 [4, 384, 768], P('dp', 'seq')
- dx_coarse: float32 [4, 192, 768], P('dp', 'seq')
- grad_attn_in: float32 [6912, 768], P(('dp', 'seq'))
- grad_attn_out: float32 [2304, 768], P(('dp', 'seq'))
- grad_mlp: float32 [4608, 3072], P(('dp', 'seq'))
- grad_cross_in: float32 [4608, 768], P(('dp', 'seq'))
- grad_cross_out: float32 [1536, 768], P(('dp', 'seq'))
- grad_gains: float32 [10, 768], P(None, ('dp', 'seq'))
- grad_biases: float32 [28, 768], P(None, ('dp', 'seq'))
- grad_ffn_bias: float32 [3, 3072], P(None, ('dp', 'seq'))
Inputs may be any that keep to these rules, and one draw needn't show every extreme that they name: `clip_ids`: along a row the ids never fall; each of the 4 clips holds 1 to 144 cells and one holds exactly 144; a cell is one coarse token, two middle tokens and four fine tokens, in order.
All inputs are finite; a program needn't handle non-finite values.
Results may differ from a plain program's by a relative error of at most 0.017.
Values may be sent and summed in bfloat16 or wider, within the bound.
No kernel may reach another device: no remote copies, remote signals or barrier semaphores. Data moves between devices by JAX's collectives and lax.ppermute only.
A program may use at most 384 MiB of HBM per device.

v0:
```python
from functools import partial

import jax
import jax.numpy as jnp
from jax import lax
from jax.sharding import PartitionSpec as P

D = 768
HEADS = 12
HEAD_DIM = 64


eps_norm = 1e-06
neg_large = -1e30


def normed(tokens, gain_row, shift_row):
    centre = jnp.mean(tokens, axis=-1, keepdims=True)
    spread = tokens - centre
    variance = jnp.mean(spread * spread, axis=-1, keepdims=True)
    return spread * lax.rsqrt(variance + eps_norm) * gain_row + shift_row


def normed_back(tokens, gain_row, shift_row, grad_out):
    unused, pullback = jax.vjp(normed, tokens, gain_row, shift_row)
    return pullback(grad_out)


def linear(left_side, right_side):
    return jnp.dot(left_side, right_side, preferred_element_type=jnp.float32)


def linear_t(left_side, right_side):
    return lax.dot_general(
        left_side, right_side, (((1,), (1,)), ((), ())), preferred_element_type=jnp.float32
    )


def outer(left_side, right_side):
    return lax.dot_general(
        left_side, right_side, (((0,), (0,)), ((), ())), preferred_element_type=jnp.float32
    )


def column_sum(matrix):
    return jnp.sum(matrix.astype(jnp.float32), axis=0)


def block(matrix, block_index):
    return matrix[block_index * D : (block_index + 1) * D]


def heads_of(matrix):
    return matrix.reshape(matrix.shape[0], HEADS, HEAD_DIM).transpose(1, 0, 2)


def heads_join(stacked):
    return stacked.transpose(1, 0, 2).reshape(stacked.shape[1], HEADS * HEAD_DIM)


def scores_of(head_q, head_k, allowed):
    scores = linear_t(head_q, head_k) * HEAD_DIM ** (-0.5)
    return jnp.where(allowed, scores, neg_large)


def attend(queries, keys_all, values_all, allowed):

    def one_head(pieces):
        head_q, head_k, head_v = pieces
        scores = scores_of(head_q, head_k, allowed)
        highest = jnp.max(scores, axis=1, keepdims=True)
        exponent = jnp.exp(scores - highest)
        row_total = jnp.sum(exponent, axis=1, keepdims=True)
        probability = (exponent / row_total).astype(jnp.bfloat16)
        return (linear(probability, head_v).astype(jnp.bfloat16), highest, row_total)

    head_outs, highest, row_total = lax.map(
        one_head, (heads_of(queries), heads_of(keys_all), heads_of(values_all))
    )
    return (heads_join(head_outs), (highest, row_total))


def attend_back(queries, keys_all, values_all, allowed, soft_stats, grad_att):

    def one_head(pieces):
        head_q, head_k, head_v, head_g, highest, row_total = pieces
        scores = scores_of(head_q, head_k, allowed)
        probability = jnp.exp(scores - highest) / row_total
        grad_prob = linear_t(head_g, head_v)
        row_delta = jnp.sum(grad_prob * probability, axis=1, keepdims=True)
        grad_scores = (probability * (grad_prob - row_delta)).astype(jnp.bfloat16)
        grad_query = linear(grad_scores, head_k) * HEAD_DIM ** (-0.5)
        grad_key = outer(grad_scores, head_q) * HEAD_DIM ** (-0.5)
        grad_value = outer(probability.astype(jnp.bfloat16), head_g)
        return (grad_query, grad_key, grad_value)

    grad_query, grad_key, grad_value = lax.map(
        one_head,
        (
            heads_of(queries),
            heads_of(keys_all),
            heads_of(values_all),
            heads_of(grad_att),
            soft_stats[0],
            soft_stats[1],
        ),
    )
    return (heads_join(grad_query), heads_join(grad_key), heads_join(grad_value))


def unpack(weights):
    return weights[:5] + (
        weights[5].astype(jnp.float32),
        weights[6].astype(jnp.float32),
        weights[7].astype(jnp.float32),
    )


def per_device(
    view_fine,
    view_mid,
    view_coarse,
    grad_fine,
    grad_mid,
    grad_coarse,
    clip_ids,
    attn_in,
    attn_out,
    mlp_w,
    cross_in,
    cross_out,
    norm_gains,
    biases,
    ffn_bias,
):
    factors = (4, 2, 1)
    inputs = (view_fine[0], view_mid[0], view_coarse[0])
    cotangents = (grad_fine[0], grad_mid[0], grad_coarse[0])
    seq_index = lax.axis_index("seq")
    full_ids = [jnp.repeat(clip_ids[0], factor) for factor in factors]
    local_ids = [
        lax.dynamic_slice_in_dim(
            full_ids[view_index],
            seq_index * inputs[view_index].shape[0],
            inputs[view_index].shape[0],
        )
        for view_index in range(3)
    ]
    self_masks = [
        local_ids[view_index][:, None] == full_ids[view_index][None, :] for view_index in range(3)
    ]
    cross_masks = [
        local_ids[pair_index + 1][:, None] == full_ids[pair_index][None, :]
        for pair_index in range(2)
    ]
    weights = (
        lax.all_gather(attn_in, ("dp", "seq"), axis=0, tiled=True),
        lax.all_gather(attn_out, ("dp", "seq"), axis=0, tiled=True),
        lax.all_gather(mlp_w, ("dp", "seq"), axis=0, tiled=True),
        lax.all_gather(cross_in, ("dp", "seq"), axis=0, tiled=True),
        lax.all_gather(cross_out, ("dp", "seq"), axis=0, tiled=True),
        lax.all_gather(norm_gains, ("dp", "seq"), axis=1, tiled=True),
        lax.all_gather(biases, ("dp", "seq"), axis=1, tiled=True),
        lax.all_gather(ffn_bias, ("dp", "seq"), axis=1, tiled=True),
    )
    attn_w, out_w, mlp_full, cross_w, cross_o, gains, vectors, ffn_rows = unpack(weights)
    saved = []
    key_parts = []
    for view_index in range(3):
        tokens = inputs[view_index].astype(jnp.float32)
        offset = 6 * view_index
        normal_a = normed(tokens, gains[2 * view_index], vectors[offset]).astype(jnp.bfloat16)
        queries = (linear(normal_a, block(attn_w, 3 * view_index)) + vectors[offset + 1]).astype(
            jnp.bfloat16
        )
        key_part = linear(normal_a, block(attn_w, 3 * view_index + 1)).astype(jnp.bfloat16)
        value_part = (
            linear(normal_a, block(attn_w, 3 * view_index + 2)) + vectors[offset + 2]
        ).astype(jnp.bfloat16)
        saved.append([tokens, normal_a, queries])
        key_parts.append((key_part, value_part))
    self_full = (
        lax.all_gather(key_parts[0][0], "seq", axis=0, tiled=True),
        lax.all_gather(key_parts[0][1], "seq", axis=0, tiled=True),
        lax.all_gather(key_parts[1][0], "seq", axis=0, tiled=True),
        lax.all_gather(key_parts[1][1], "seq", axis=0, tiled=True),
        lax.all_gather(key_parts[2][0], "seq", axis=0, tiled=True),
        lax.all_gather(key_parts[2][1], "seq", axis=0, tiled=True),
    )
    encoded = []
    for view_index in range(3):
        tokens, normal_a, queries = saved[view_index]
        offset = 6 * view_index
        attended, soft_stats = attend(
            queries,
            self_full[2 * view_index],
            self_full[2 * view_index + 1],
            self_masks[view_index],
        )
        hidden = tokens + (linear(attended, block(out_w, view_index)) + vectors[offset + 3])
        normal_c = normed(hidden, gains[2 * view_index + 1], vectors[offset + 4]).astype(
            jnp.bfloat16
        )
        inner_sum = linear(normal_c, block(mlp_full, 2 * view_index)) + ffn_rows[view_index]
        activated = jax.nn.gelu(inner_sum, approximate=False).astype(jnp.bfloat16)
        encoded.append(
            hidden
            + (linear_t(activated, block(mlp_full, 2 * view_index + 1)) + vectors[offset + 5])
        )
        saved[view_index] = saved[view_index] + [
            attended,
            soft_stats,
            hidden,
            normal_c,
            inner_sum,
            activated,
        ]
    cross_saved = []
    cross_parts = []
    for pair_index in range(2):
        offset = 18 + 5 * pair_index
        normal_q = normed(
            encoded[pair_index + 1], gains[6 + 2 * pair_index], vectors[offset]
        ).astype(jnp.bfloat16)
        normal_k = normed(
            encoded[pair_index], gains[7 + 2 * pair_index], vectors[offset + 1]
        ).astype(jnp.bfloat16)
        queries = (linear(normal_q, block(cross_w, 3 * pair_index)) + vectors[offset + 2]).astype(
            jnp.bfloat16
        )
        key_part = linear(normal_k, block(cross_w, 3 * pair_index + 1)).astype(jnp.bfloat16)
        value_part = (
            linear(normal_k, block(cross_w, 3 * pair_index + 2)) + vectors[offset + 3]
        ).astype(jnp.bfloat16)
        cross_saved.append([normal_q, normal_k, queries])
        cross_parts.append((key_part, value_part))
    cross_full = (
        lax.all_gather(cross_parts[0][0], "seq", axis=0, tiled=True),
        lax.all_gather(cross_parts[0][1], "seq", axis=0, tiled=True),
        lax.all_gather(cross_parts[1][0], "seq", axis=0, tiled=True),
        lax.all_gather(cross_parts[1][1], "seq", axis=0, tiled=True),
    )
    mixed = []
    for pair_index in range(2):
        normal_q, normal_k, queries = cross_saved[pair_index]
        attended, soft_stats = attend(
            queries,
            cross_full[2 * pair_index],
            cross_full[2 * pair_index + 1],
            cross_masks[pair_index],
        )
        mixed.append(
            encoded[pair_index + 1]
            + (linear(attended, block(cross_o, pair_index)) + vectors[18 + 5 * pair_index + 4])
        )
        cross_saved[pair_index] = cross_saved[pair_index] + [attended, soft_stats]
    weights_back = (
        lax.all_gather(attn_in, ("dp", "seq"), axis=0, tiled=True),
        lax.all_gather(attn_out, ("dp", "seq"), axis=0, tiled=True),
        lax.all_gather(mlp_w, ("dp", "seq"), axis=0, tiled=True),
        lax.all_gather(cross_in, ("dp", "seq"), axis=0, tiled=True),
        lax.all_gather(cross_out, ("dp", "seq"), axis=0, tiled=True),
        lax.all_gather(norm_gains, ("dp", "seq"), axis=1, tiled=True),
        lax.all_gather(biases, ("dp", "seq"), axis=1, tiled=True),
        lax.all_gather(ffn_bias, ("dp", "seq"), axis=1, tiled=True),
    )
    attn_w, out_w, mlp_full, cross_w, cross_o, gains, vectors, ffn_rows = unpack(weights_back)
    cross_back = (
        lax.all_gather(cross_parts[0][0], "seq", axis=0, tiled=True),
        lax.all_gather(cross_parts[0][1], "seq", axis=0, tiled=True),
        lax.all_gather(cross_parts[1][0], "seq", axis=0, tiled=True),
        lax.all_gather(cross_parts[1][1], "seq", axis=0, tiled=True),
    )
    gain_grads = [None] * 10
    bias_grads = [None] * 28
    cross_in_grads = [None] * 6
    cross_out_grads = [None] * 2
    grad_rows = [cotangents[view_index].astype(jnp.float32) for view_index in range(3)]
    cross_partials = []
    for pair_index in range(2):
        normal_q, normal_k, queries, attended, soft_stats = cross_saved[pair_index]
        grad_branch = cotangents[pair_index + 1]
        cross_out_grads[pair_index] = outer(attended, grad_branch)
        bias_grads[18 + 5 * pair_index + 4] = column_sum(grad_branch)
        grad_att = linear_t(grad_branch, block(cross_o, pair_index)).astype(jnp.bfloat16)
        cross_partials.append(
            attend_back(
                queries,
                cross_back[2 * pair_index],
                cross_back[2 * pair_index + 1],
                cross_masks[pair_index],
                soft_stats,
                grad_att,
            )
        )
    cross_sums = (
        lax.psum_scatter(
            cross_partials[0][1].astype(jnp.bfloat16), "seq", scatter_dimension=0, tiled=True
        ).astype(jnp.float32),
        lax.psum_scatter(
            cross_partials[0][2].astype(jnp.bfloat16), "seq", scatter_dimension=0, tiled=True
        ).astype(jnp.float32),
        lax.psum_scatter(
            cross_partials[1][1].astype(jnp.bfloat16), "seq", scatter_dimension=0, tiled=True
        ).astype(jnp.float32),
        lax.psum_scatter(
            cross_partials[1][2].astype(jnp.bfloat16), "seq", scatter_dimension=0, tiled=True
        ).astype(jnp.float32),
    )
    for pair_index in range(2):
        normal_q, normal_k, queries, attended, soft_stats = cross_saved[pair_index]
        offset = 18 + 5 * pair_index
        grad_query = cross_partials[pair_index][0].astype(jnp.bfloat16)
        grad_key = cross_sums[2 * pair_index].astype(jnp.bfloat16)
        grad_value = cross_sums[2 * pair_index + 1].astype(jnp.bfloat16)
        cross_in_grads[3 * pair_index] = outer(normal_q, grad_query)
        cross_in_grads[3 * pair_index + 1] = outer(normal_k, grad_key)
        cross_in_grads[3 * pair_index + 2] = outer(normal_k, grad_value)
        bias_grads[offset + 2] = column_sum(grad_query)
        bias_grads[offset + 3] = column_sum(grad_value)
        grad_normal_q = linear_t(grad_query, block(cross_w, 3 * pair_index))
        from_query, gain_grads[6 + 2 * pair_index], bias_grads[offset] = normed_back(
            encoded[pair_index + 1], gains[6 + 2 * pair_index], vectors[offset], grad_normal_q
        )
        grad_normal_k = linear_t(grad_key, block(cross_w, 3 * pair_index + 1)) + linear_t(
            grad_value, block(cross_w, 3 * pair_index + 2)
        )
        from_key, gain_grads[7 + 2 * pair_index], bias_grads[offset + 1] = normed_back(
            encoded[pair_index], gains[7 + 2 * pair_index], vectors[offset + 1], grad_normal_k
        )
        grad_rows[pair_index + 1] = grad_rows[pair_index + 1] + from_query
        grad_rows[pair_index] = grad_rows[pair_index] + from_key
    self_back = (
        lax.all_gather(key_parts[0][0], "seq", axis=0, tiled=True),
        lax.all_gather(key_parts[0][1], "seq", axis=0, tiled=True),
        lax.all_gather(key_parts[1][0], "seq", axis=0, tiled=True),
        lax.all_gather(key_parts[1][1], "seq", axis=0, tiled=True),
        lax.all_gather(key_parts[2][0], "seq", axis=0, tiled=True),
        lax.all_gather(key_parts[2][1], "seq", axis=0, tiled=True),
    )
    attn_in_grads = [None] * 9
    attn_out_grads = [None] * 3
    mlp_grads = [None] * 6
    ffn_grads = [None] * 3
    self_partials = []
    grad_hiddens = []
    for view_index in range(3):
        tokens, normal_a, queries, attended, soft_stats, hidden, normal_c, inner_sum, activated = (
            saved[view_index]
        )
        offset = 6 * view_index
        grad_mlp_out = grad_rows[view_index].astype(jnp.bfloat16)
        mlp_grads[2 * view_index + 1] = outer(grad_mlp_out, activated)
        bias_grads[offset + 5] = column_sum(grad_mlp_out)
        grad_act = linear(grad_mlp_out, block(mlp_full, 2 * view_index + 1))
        unused, gelu_pull = jax.vjp(partial(jax.nn.gelu, approximate=False), inner_sum)
        grad_inner = gelu_pull(grad_act)[0].astype(jnp.bfloat16)
        mlp_grads[2 * view_index] = outer(normal_c, grad_inner)
        ffn_grads[view_index] = column_sum(grad_inner)
        grad_normal_c = linear_t(grad_inner, block(mlp_full, 2 * view_index))
        from_norm, gain_grads[2 * view_index + 1], bias_grads[offset + 4] = normed_back(
            hidden, gains[2 * view_index + 1], vectors[offset + 4], grad_normal_c
        )
        grad_hidden = grad_rows[view_index] + from_norm
        grad_hiddens.append(grad_hidden)
        grad_branch = grad_hidden.astype(jnp.bfloat16)
        attn_out_grads[view_index] = outer(attended, grad_branch)
        bias_grads[offset + 3] = column_sum(grad_branch)
        grad_att = linear_t(grad_branch, block(out_w, view_index)).astype(jnp.bfloat16)
        self_partials.append(
            attend_back(
                queries,
                self_back[2 * view_index],
                self_back[2 * view_index + 1],
                self_masks[view_index],
                soft_stats,
                grad_att,
            )
        )
    self_sums = (
        lax.psum_scatter(
            self_partials[0][1].astype(jnp.bfloat16), "seq", scatter_dimension=0, tiled=True
        ).astype(jnp.float32),
        lax.psum_scatter(
            self_partials[0][2].astype(jnp.bfloat16), "seq", scatter_dimension=0, tiled=True
        ).astype(jnp.float32),
        lax.psum_scatter(
            self_partials[1][1].astype(jnp.bfloat16), "seq", scatter_dimension=0, tiled=True
        ).astype(jnp.float32),
        lax.psum_scatter(
            self_partials[1][2].astype(jnp.bfloat16), "seq", scatter_dimension=0, tiled=True
        ).astype(jnp.float32),
        lax.psum_scatter(
            self_partials[2][1].astype(jnp.bfloat16), "seq", scatter_dimension=0, tiled=True
        ).astype(jnp.float32),
        lax.psum_scatter(
            self_partials[2][2].astype(jnp.bfloat16), "seq", scatter_dimension=0, tiled=True
        ).astype(jnp.float32),
    )
    input_grads = []
    for view_index in range(3):
        tokens, normal_a = (saved[view_index][0], saved[view_index][1])
        offset = 6 * view_index
        grad_query = self_partials[view_index][0].astype(jnp.bfloat16)
        grad_key = self_sums[2 * view_index].astype(jnp.bfloat16)
        grad_value = self_sums[2 * view_index + 1].astype(jnp.bfloat16)
        attn_in_grads[3 * view_index] = outer(normal_a, grad_query)
        attn_in_grads[3 * view_index + 1] = outer(normal_a, grad_key)
        attn_in_grads[3 * view_index + 2] = outer(normal_a, grad_value)
        bias_grads[offset + 1] = column_sum(grad_query)
        bias_grads[offset + 2] = column_sum(grad_value)
        grad_normal_a = (
            linear_t(grad_query, block(attn_w, 3 * view_index))
            + linear_t(grad_key, block(attn_w, 3 * view_index + 1))
            + linear_t(grad_value, block(attn_w, 3 * view_index + 2))
        )
        from_norm, gain_grads[2 * view_index], bias_grads[offset] = normed_back(
            tokens, gains[2 * view_index], vectors[offset], grad_normal_a
        )
        input_grads.append(grad_hiddens[view_index] + from_norm)
    g_attn_in = jnp.concatenate(attn_in_grads, axis=0)
    g_attn_out = jnp.concatenate(attn_out_grads, axis=0)
    g_mlp = jnp.concatenate(mlp_grads, axis=0)
    g_cross_in = jnp.concatenate(cross_in_grads, axis=0)
    g_cross_out = jnp.concatenate(cross_out_grads, axis=0)
    g_gains = jnp.stack(gain_grads, axis=0)
    g_biases = jnp.stack(bias_grads, axis=0)
    g_ffn = jnp.stack(ffn_grads, axis=0)
    shards = (
        lax.psum_scatter(g_attn_in, ("dp", "seq"), scatter_dimension=0, tiled=True),
        lax.psum_scatter(g_attn_out, ("dp", "seq"), scatter_dimension=0, tiled=True),
        lax.psum_scatter(g_mlp, ("dp", "seq"), scatter_dimension=0, tiled=True),
        lax.psum_scatter(g_cross_in, ("dp", "seq"), scatter_dimension=0, tiled=True),
        lax.psum_scatter(g_cross_out, ("dp", "seq"), scatter_dimension=0, tiled=True),
        lax.psum_scatter(g_gains, ("dp", "seq"), scatter_dimension=1, tiled=True),
        lax.psum_scatter(g_biases, ("dp", "seq"), scatter_dimension=1, tiled=True),
        lax.psum_scatter(g_ffn, ("dp", "seq"), scatter_dimension=1, tiled=True),
    )
    return (
        encoded[0].astype(jnp.bfloat16)[None],
        mixed[0].astype(jnp.bfloat16)[None],
        mixed[1].astype(jnp.bfloat16)[None],
        input_grads[0][None],
        input_grads[1][None],
        input_grads[2][None],
        shards[0],
        shards[1],
        shards[2],
        shards[3],
        shards[4],
        shards[5],
        shards[6],
        shards[7],
    )


def solution(mesh):
    return jax.shard_map(
        per_device,
        mesh=mesh,
        in_specs=(
            P("dp", "seq", None),
            P("dp", "seq", None),
            P("dp", "seq", None),
            P("dp", "seq", None),
            P("dp", "seq", None),
            P("dp", "seq", None),
            P("dp", None),
            P(("dp", "seq"), None),
            P(("dp", "seq"), None),
            P(("dp", "seq"), None),
            P(("dp", "seq"), None),
            P(("dp", "seq"), None),
            P(None, ("dp", "seq")),
            P(None, ("dp", "seq")),
            P(None, ("dp", "seq")),
        ),
        out_specs=(
            P("dp", "seq", None),
            P("dp", "seq", None),
            P("dp", "seq", None),
            P("dp", "seq", None),
            P("dp", "seq", None),
            P("dp", "seq", None),
            P(("dp", "seq"), None),
            P(("dp", "seq"), None),
            P(("dp", "seq"), None),
            P(("dp", "seq"), None),
            P(("dp", "seq"), None),
            P(None, ("dp", "seq")),
            P(None, ("dp", "seq")),
            P(None, ("dp", "seq")),
        ),
        check_vma=False,
    )
```

profile of v0, /device:TPU:0, one launch (start us, length us, event | category | flops | bytes accessed | tf_op | source)
XLA Modules:
  0.0 2610.4 jit_solution(2178254137829470173)
XLA Ops:
  9.5 44.4 %all-gather = bf16[32,24,10]{1,2,0:T(8,128)(2,1)S(1)} all-gather(bf16[1,24,10]{1,2,0:T(8,128)(2,1)} %bitcast.901), channel_id=1, replica_groups=mesh['dp'=4,'seq'=8] {'dp','seq'}, dimensions={0}, use_global_device_ids=true | all-gather | bytes 15840 | tf_op jit(solution)/shard_map/all_gather | solution.py:162
  54.2 38.3 %all_gather.71 = bf16[28,768]{0,1:T(8,128)(2,1)S(1)} all-gather(bf16[28,24]{0,1:T(8,128)(2,1)S(1)} %copy-done.191), channel_id=1, replica_groups=mesh['dp'=4,'seq'=8] {'dp','seq'}, dimensions={1}, use_global_device_ids=true | all-gather | bytes 44352 | tf_op jit(solution)/shard_map/all_gather | solution.py:163
  95.9 5.9 all-gather.12.cloned.1.call-done
  108.0 4.5 slice_reduce_fusion
  113.3 39.4 %all-gather.1 = bf16[32,96,3]{1,2,0:T(4,128)(2,1)S(1)} all-gather(bf16[1,96,3]{1,2,0:T(4,128)(2,1)S(1)} %bitcast.902), channel_id=1, replica_groups=mesh['dp'=4,'seq'=8] {'dp','seq'}, dimensions={0}, use_global_device_ids=true | all-gather | bytes 19008 | tf_op jit(solution)/shard_map/all_gather | solution.py:164
  155.3 6.0 all-gather.28.cloned.1.call-done
  173.7 9.4 all_gather.84
  185.3 9.6 all_gather.85
  195.4 8.5 while.153
  206.4 11.5 all_gather.78
  220.7 10.0 all_gather.79
  233.4 8.6 while.151
  247.4 4.0 all-gather.14.cloned.1.call-done
  253.8 2.8 copy.171
  256.5 21.2 all-gather.16.cloned.1.call-done
  280.1 3.8 copy.172
  283.9 28.0 %while.150 = (s32[]{:T(128)}, bf16[12,96,64]{1,2,0:T(8,128)(2,1)S(1)}, f32[12,96,1]{1,2,0:T(1,128)}, f32[12,96,1]{1,2,0:T(1,128)}, bf16[12,96,64]{2,1,0:T(8,128)...) while((s32[]{:T(128)}, ...), condition=%wide.region_5.0_spmd.clone, body=%wide.region_2.5_spmd.clone.sunk | while | flops 19543872 | bytes 1329649 | solution.py:77
  315.1 135.1 %all-gather.20.cloned.1.call-done = bf16[4608,3072]{1,0:T(8,128)(2,1)} async-done(((bf16[144,3072]{1,0:T(8,128)(2,1)}), bf16[4608,3072]{1,0:T(8,128)(2,1)}) %all-gather.20.cloned.1.call-update) | async-done | bytes 28311568 | tf_op jit(solution)/shard_map/all_gather | solution.py:159
  450.3 3.1 fusion.280
  453.4 4.3 fusion.529
  458.0 65.8 %all-gather.22.cloned.1.call-done = bf16[4608,768]{1,0:T(8,128)(2,1)} async-done(((bf16[144,768]{1,0:T(8,128)(2,1)}), bf16[4608,768]{1,0:T(8,128)(2,1)}) %all-gather.22.cloned.1.call-update) | async-done | bytes 7077904 | tf_op jit(solution)/shard_map/all_gather | solution.py:160
  526.3 3.3 fusion.277
  529.7 5.0 fusion.525
  537.3 10.9 all_gather.86
  551.9 10.5 all_gather.87
  569.2 3.3 fusion.274
  572.6 5.9 fusion.527
  583.1 36.0 %while.154 = (s32[]{:T(128)}, bf16[12,24,64]{2,1,0:T(8,128)(2,1)S(1)}, f32[12,24,1]{1,2,0:T(1,128)}, f32[12,24,1]{1,2,0:T(1,128)S(1)}, bf16[12,24,64]{2,1,0:T(8,...) while((s32[]{:T(128)}, ...), condition=%wide.region_37.38_spmd.clone, body=%wide.region_34.37_spmd.clone.sunk | while | flops 2443730 | bytes 327057 | solution.py:77
  623.3 85.1 %while.157 = (s32[]{:T(128)}, bf16[12,24,64]{2,1,0:T(8,128)(2,1)S(1)}, bf16[12,384,64]{1,2,0:T(8,128)(2,1)}, bf16[12,384,64]{1,2,0:T(8,128)(2,1)}, bf16[12,24,64...) while((s32[]{:T(128)}, ...), condition=%wide.region_58.59_spmd.clone, body=%wide.region_56.58_spmd.clone.sunk | while | flops 6025706 | bytes 812521 | solution.py:97
  722.8 3.7 copy.183
  728.9 3.7 copy.184
  732.7 32.2 %while.152 = (s32[]{:T(128)}, bf16[12,48,64]{2,1,0:T(8,128)(2,1)S(1)}, f32[12,48,1]{1,2,0:T(1,128)S(1)}, f32[12,48,1]{1,2,0:T(1,128)S(1)}, bf16[12,48,64]{2,1,0:...) while((s32[]{:T(128)}, ...), condition=%wide.region_23.24_spmd.clone, body=%wide.region_20.23_spmd.clone.sunk | while | flops 9771938 | bytes 869233 | solution.py:77
  767.8 81.3 %while.155 = (s32[]{:T(128)}, bf16[12,48,64]{2,1,0:T(8,128)(2,1)S(1)}, bf16[12,768,64]{1,2,0:T(8,128)(2,1)}, bf16[12,768,64]{1,2,0:T(8,128)(2,1)}, bf16[12,48,64...) while((s32[]{:T(128)}, ...), condition=%wide.region_40.41_spmd.clone, body=%wide.region_38.40_spmd.clone.sunk | while | flops 24050640 | bytes 2172745 | solution.py:97
  851.8 4.2 convert_reduce_fusion.9
  856.1 4.5 multiply_reduce_fusion.20
  867.1 81.6 %while.159 = (s32[]{:T(128)}, bf16[12,24,64]{2,1,0:T(8,128)(2,1)S(1)}, bf16[12,192,64]{1,2,0:T(8,128)(2,1)}, bf16[12,192,64]{1,2,0:T(8,128)(2,1)}, bf16[12,24,64...) while((s32[]{:T(128)}, ...), condition=%wide.region_78.79_spmd.clone, body=%wide.region_76.78_spmd.clone.sunk | while | flops 3013610 | bytes 463593 | solution.py:97
  962.4 5.1 convert_reduce_fusion.1
  967.6 4.6 multiply_reduce_fusion.13
  979.3 85.5 %while.158 = (s32[]{:T(128)}, bf16[12,48,64]{2,1,0:T(8,128)(2,1)S(1)}, bf16[12,384,64]{1,2,0:T(8,128)(2,1)}, bf16[12,384,64]{1,2,0:T(8,128)(2,1)}, bf16[12,48,64...) while((s32[]{:T(128)}, ...), condition=%wide.region_67.68_spmd.clone, body=%wide.region_65.67_spmd.clone.sunk | while | flops 12026834 | bytes 1127049 | solution.py:97
  1071.1 2.6 fusion.352
  1077.9 6.5 convert_reduce_fusion
  1084.4 4.9 multiply_reduce_fusion.6
  1096.6 84.1 %while.156 = (s32[]{:T(128)}, bf16[12,96,64]{1,2,0:T(8,128)(2,1)}, bf16[12,768,64]{1,2,0:T(8,128)(2,1)}, bf16[12,768,64]{1,2,0:T(8,128)(2,1)}, bf16[12,96,64]{2,...) while((s32[]{:T(128)}, bf16[12,96,64]{1,2,0:T(8,128)(2,1)}, ...), condition=%wide.region_49.50_spmd.clone, body=%wide.region_47.49_spmd.clone.sunk | while | flops 48052128 | bytes 3322761 | solution.py:97
  1195.2 3.0 fusion.506
  1236.2 3.1 fusion.505
  1257.6 2.6 fusion.369
  1263.9 3.2 fusion.504
  1267.8 5.4 stack.111
  1273.2 4.1 pad_maximum_fusion.1
  1280.1 3.3 pad_maximum_fusion
  1316.2 5.1 convolution_dynamic-update-slice_fusion.1
  1321.4 5.7 convolution_dynamic-update-slice_fusion
  1327.1 5.2 convolution_dynamic-update-slice_fusion.5
  1332.4 5.3 convolution_dynamic-update-slice_fusion.4
  1337.8 5.1 convolution_dynamic-update-slice_fusion.3
  1342.9 5.1 convolution_dynamic-update-slice_fusion.2
  1354.8 9.3 reduce-scatter.71.cloned.1.call-done
  1365.9 40.4 %all-reduce = f32[10,768]{1,0:T(8,128)S(1)} all-reduce(f32[10,768]{1,0:T(8,128)S(1)} %stack.92), channel_id=17, replica_groups=mesh['dp'=4,'seq'=8] {'dp','seq'}, use_global_device_ids=true, to_apply=%region_98.99.clone | all-reduce | flops 7680 | bytes 61440
  1407.9 81.4 %all-reduce.4.cloned.1.call-done = f32[28,768]{1,0:T(8,128)} async-done(((f32[28,768]{1,0:T(8,128)}), f32[28,768]{1,0:T(8,128)}) %all-reduce.4.cloned.1.call-update) | async-done | bytes 86032
  1490.8 112.4 %reduce-scatter.49.cloned.1.call-done = f32[48,768]{1,0:T(8,128)} async-done(((f32[1536,768]{1,0:T(8,128)}), f32[48,768]{1,0:T(8,128)}) %reduce-scatter.49.cloned.1.call-update) | async-done | bytes 147472 | tf_op jit(solution)/shard_map/reduce_scatter | solution.py:434
  1603.2 125.3 %reduce-scatter.43.cloned.1.call-done = f32[72,768]{1,0:T(8,128)} async-done(((f32[2304,768]{1,0:T(8,128)}), f32[72,768]{1,0:T(8,128)}) %reduce-scatter.43.cloned.1.call-update) | async-done | bytes 221200 | tf_op jit(solution)/shard_map/reduce_scatter | solution.py:431
  1728.6 168.6 %reduce-scatter.47.cloned.1.call-done = f32[144,768]{1,0:T(8,128)} async-done(((f32[4608,768]{1,0:T(8,128)}), f32[144,768]{1,0:T(8,128)}) %reduce-scatter.47.cloned.1.call-update) | async-done | bytes 442384 | tf_op jit(solution)/shard_map/reduce_scatter | solution.py:433
  1897.2 225.6 %reduce-scatter.41.cloned.1.call-done = f32[216,768]{1,0:T(8,128)} async-done(((f32[6912,768]{1,0:T(8,128)}), f32[216,768]{1,0:T(8,128)}) %reduce-scatter.41.cloned.1.call-update) | async-done | bytes 663568 | tf_op jit(solution)/shard_map/reduce_scatter | solution.py:430
  2122.8 480.9 %reduce-scatter.45.cloned.1.call-done = f32[144,3072]{1,0:T(8,128)} async-done(((f32[4608,3072]{1,0:T(8,128)}), f32[144,3072]{1,0:T(8,128)}) %reduce-scatter.45.cloned.1.call-update) | async-done | bytes 1769488 | tf_op jit(solution)/shard_map/reduce_scatter | solution.py:432
  (1536 shorter events, 792.3 us)
Async XLA Ops:
  7.2 85.4 %copy-start = (bf16[1,96,768]{2,1,0:T(8,128)(2,1)S(1)}, bf16[1,96,768]{2,1,0:T(8,128)(2,1)}, u32[]{:S(2)}) copy-start(bf16[1,96,768]{2,1,0:T(8,128)(2,1)} %param.35) | copy-start | bytes 442372
  7.2 94.6 %all-gather.12.cloned.1.call-start = ((), (), s32[]{:S(2)}) async-start(), calls=%async_computation.16 | async-start | bytes 10948608 | tf_op jit(solution)/shard_map/all_gather | solution.py:157
  7.9 153.3 %all-gather.28.cloned.1.call-start = ((), (), s32[]{:S(2)}) async-start(), calls=%async_computation.24 | async-start | bytes 2433024 | tf_op jit(solution)/shard_map/all_gather | solution.py:161
  8.7 233.6 %all-gather.18.cloned.1.call-start = ((), (), s32[]{:S(2)}) async-start(), calls=%async_computation.19 | async-start | bytes 3649536 | tf_op jit(solution)/shard_map/all_gather | solution.py:158
  9.4 242.0 %all-gather.14.cloned.1.call-start = ((), (), s32[]{:S(2)}) async-start(), calls=%async_computation.17 | async-start | bytes 1327104 | tf_op jit(solution)/shard_map/all_gather | solution.py:183
  93.4 90.3 %copy-start.86 = (f32[768]{0:T(1024)}, f32[768]{0:T(1024)S(1)}, u32[]{:S(2)}) copy-start(f32[768]{0:T(1024)S(1)} %get-tuple-element.1232) | copy-start | bytes 9220
  93.4 76.7 %copy-start.131 = (f32[96]{0:T(128)}, f32[96]{0:T(128)S(1)}, u32[]{:S(2)}) copy-start(f32[96]{0:T(128)S(1)} %broadcast_multiply_fusion.8) | copy-start | bytes 1156
  95.9 74.2 %copy-start.111 = (f32[768]{0:T(1024)}, f32[768]{0:T(1024)S(1)}, u32[]{:S(2)}) copy-start(f32[768]{0:T(1024)S(1)} %get-tuple-element.1199) | copy-start | bytes 9220
  95.9 123.1 %copy-start.109 = (f32[768]{0:T(1024)}, f32[768]{0:T(1024)S(1)}, u32[]{:S(2)}) copy-start(f32[768]{0:T(1024)S(1)} %get-tuple-element.1193) | copy-start | bytes 9220
  95.9 74.2 %copy-start.156 = (f32[96]{0:T(128)}, f32[96]{0:T(128)S(1)}, u32[]{:S(2)}) copy-start(f32[96]{0:T(128)S(1)} %fusion.469) | copy-start | bytes 1156
  104.2 173.6 %all-gather.16.cloned.1.call-start = ((), (), s32[]{:S(2)}) async-start(), calls=%async_computation.18 | async-start | bytes 1327104 | tf_op jit(solution)/shard_map/all_gather | solution.py:184
  106.6 343.7 %all-gather.20.cloned.1.call-start = ((), (), s32[]{:S(2)}) async-start(), calls=%async_computation.20 | async-start | bytes 29196288 | tf_op jit(solution)/shard_map/all_gather | solution.py:159
  107.1 416.7 %all-gather.22.cloned.1.call-start = ((), (), s32[]{:S(2)}) async-start(), calls=%async_computation.21 | async-start | bytes 7299072 | tf_op jit(solution)/shard_map/all_gather | solution.py:160
  107.9 612.5 %all-gather.24.cloned.1.call-start = ((), (), s32[]{:S(2)}) async-start(), calls=%async_computation.22 | async-start | bytes 1327104 | tf_op jit(solution)/shard_map/all_gather | solution.py:238
  108.0 53.3 %copy-start.58 = (bf16[1,24,768]{2,1,0:T(8,128)(2,1)S(1)}, bf16[1,24,768]{2,1,0:T(8,128)(2,1)}, u32[]{:S(2)}) copy-start(bf16[1,24,768]{2,1,0:T(8,128)(2,1)} %param.40) | copy-start | bytes 110596
  112.5 71.1 %copy-start.107 = (f32[768]{0:T(1024)}, f32[768]{0:T(1024)S(1)}, u32[]{:S(2)}) copy-start(f32[768]{0:T(1024)S(1)} %get-tuple-element.1182) | copy-start | bytes 9220
  112.7 106.3 %copy-start.135 = (f32[48]{0:T(128)}, f32[48]{0:T(128)S(1)}, u32[]{:S(2)}) copy-start(f32[48]{0:T(128)S(1)} %broadcast_multiply_fusion.5) | copy-start | bytes 580
  112.9 50.9 %copy-start.71 = (bf16[1,48,768]{2,1,0:T(8,128)(2,1)S(1)}, bf16[1,48,768]{2,1,0:T(8,128)(2,1)}, u32[]{:S(2)}) copy-start(bf16[1,48,768]{2,1,0:T(8,128)(2,1)} %param.39) | copy-start | bytes 221188
  112.9 106.1 %copy-start.159 = (f32[48]{0:T(128)}, f32[48]{0:T(128)S(1)}, u32[]{:S(2)}) copy-start(f32[48]{0:T(128)S(1)} %fusion.471) | copy-start | bytes 580
  113.0 70.6 %copy-start.139 = (f32[24]{0:T(128)}, f32[24]{0:T(128)S(1)}, u32[]{:S(2)}) copy-start(f32[24]{0:T(128)S(1)} %broadcast_multiply_fusion.2) | copy-start | bytes 292
  113.3 70.4 %copy-start.162 = (f32[24]{0:T(128)}, f32[24]{0:T(128)S(1)}, u32[]{:S(2)}) copy-start(f32[24]{0:T(128)S(1)} %fusion.475) | copy-start | bytes 292
  244.6 205.6 %copy-start.166 = (f32[24]{0:T(128)}, f32[24]{0:T(128)S(1)}, u32[]{:S(2)}) copy-start(f32[24]{0:T(128)S(1)} %broadcast_multiply_fusion.1) | copy-start | bytes 292
  246.6 283.1 %copy-start.12 = (f32[48,768]{1,0:T(8,128)}, f32[48,768]{1,0:T(8,128)S(1)}, u32[]{:S(2)}) copy-start(f32[48,768]{1,0:T(8,128)S(1)} %get-tuple-element.1526) | copy-start | bytes 442372
  246.8 203.4 %copy-start.188 = (f32[24]{0:T(128)}, f32[24]{0:T(128)S(1)}, u32[]{:S(2)}) copy-start(f32[24]{0:T(128)S(1)} %fusion.476) | copy-start | bytes 292
  311.8 138.4 %copy-start.37 = (bf16[12,96,64]{1,2,0:T(8,128)(2,1)}, bf16[12,96,64]{1,2,0:T(8,128)(2,1)S(1)}, u32[]{:S(2)}) copy-start(bf16[12,96,64]{1,2,0:T(8,128)(2,1)S(1)} %get-tuple-element.529) | copy-start | bytes 442372
  311.8 138.4 %copy-start.81 = (f32[768]{0:T(1024)S(1)}, f32[768]{0:T(1024)}, u32[]{:S(2)}) copy-start(f32[768]{0:T(1024)} %get-tuple-element.1231) | copy-start | bytes 9220
  311.8 138.4 %copy-start.88 = (f32[768]{0:T(1024)S(1)}, f32[768]{0:T(1024)}, u32[]{:S(2)}) copy-start(f32[768]{0:T(1024)} %get-tuple-element.1178) | copy-start | bytes 9220
  311.8 138.4 %copy-start.121 = (f32[1,3072]{1,0:T(1,128)S(1)}, f32[1,3072]{1,0:T(1,128)}, u32[]{:S(2)}) copy-start(f32[1,3072]{1,0:T(1,128)} %get-tuple-element.1521) | copy-start | bytes 36868
  314.3 139.1 %copy-start.176 = (f32[96]{0:T(128)}, f32[96]{0:T(128)S(1)}, u32[]{:S(2)}) copy-start(f32[96]{0:T(128)S(1)} %broadcast_multiply_fusion.7) | copy-start | bytes 1156
  314.5 138.9 %copy-start.241 = (f32[96]{0:T(128)}, f32[96]{0:T(128)S(1)}, u32[]{:S(2)}) copy-start(f32[96]{0:T(128)S(1)} %multiply_reduce_fusion.10) | copy-start | bytes 1156
  457.7 261.7 %copy-start.31 = (f32[24,768]{1,0:T(8,128)}, f32[24,768]{1,0:T(8,128)S(1)}, u32[]{:S(2)}) copy-start(f32[24,768]{1,0:T(8,128)S(1)} %get-tuple-element.1537) | copy-start | bytes 221188
  457.7 68.5 %copy-start.90 = (f32[768]{0:T(1024)S(1)}, f32[768]{0:T(1024)}, u32[]{:S(2)}) copy-start(f32[768]{0:T(1024)} %get-tuple-element.1235) | copy-start | bytes 9220
  457.7 68.5 %copy-start.103 = (f32[768]{0:T(1024)S(1)}, f32[768]{0:T(1024)}, u32[]{:S(2)}) copy-start(f32[768]{0:T(1024)} %get-tuple-element.1189) | copy-start | bytes 9220
  457.7 68.5 %copy-start.175 = (f32[1,3072]{1,0:T(1,128)S(1)}, f32[1,3072]{1,0:T(1,128)}, u32[]{:S(2)}) copy-start(f32[1,3072]{1,0:T(1,128)} %get-tuple-element.1522) | copy-start | bytes 36868
  457.8 68.5 %copy-start.181 = (f32[48]{0:T(128)S(1)}, f32[48]{0:T(128)}, u32[]{:S(2)}) copy-start(f32[48]{0:T(128)} %copy-done.180) | copy-start | bytes 580
  457.8 68.5 %copy-start.195 = (f32[48]{0:T(128)S(1)}, f32[48]{0:T(128)}, u32[]{:S(2)}) copy-start(f32[48]{0:T(128)} %fusion.472) | copy-start | bytes 580
  457.8 66.1 %copy-start.198 = (f32[24]{0:T(128)}, f32[24]{0:T(128)S(1)}, u32[]{:S(2)}) copy-start(f32[24]{0:T(128)S(1)} %broadcast_multiply_fusion) | copy-start | bytes 292
  458.0 65.9 %copy-start.252 = (f32[24]{0:T(128)}, f32[24]{0:T(128)S(1)}, u32[]{:S(2)}) copy-start(f32[24]{0:T(128)S(1)} %multiply_reduce_fusion.23) | copy-start | bytes 292
  458.0 65.9 %copy-start.223 = (f32[24]{0:T(128)}, f32[24]{0:T(128)S(1)}, u32[]{:S(2)}) copy-start(f32[24]{0:T(128)S(1)} %fusion.477) | copy-start | bytes 292
  582.4 144.2 %all-gather.26.cloned.1.call-start = ((), (), s32[]{:S(2)}) async-start(), calls=%async_computation.23 | async-start | bytes 1327104 | tf_op jit(solution)/shard_map/all_gather | solution.py:239
  621.4 331.2 %reduce-scatter.59.cloned.1.call-start = ((), (), s32[]{:S(2)}) async-start(), calls=%async_computation.34 | async-start | bytes 663552
  623.3 85.2 %copy-start.124 = (f32[768]{0:T(1024)S(1)}, f32[768]{0:T(1024)}, u32[]{:S(2)}) copy-start(f32[768]{0:T(1024)} %get-tuple-element.1234) | copy-start | bytes 9220
  623.3 85.2 %copy-start.146 = (f32[768]{0:T(1024)S(1)}, f32[768]{0:T(1024)}, u32[]{:S(2)}) copy-start(f32[768]{0:T(1024)} %get-tuple-element.1187) | copy-start | bytes 9220
  623.3 85.2 %copy-start.185 = (f32[48]{0:T(128)S(1)}, f32[48]{0:T(128)}, u32[]{:S(2)}) copy-start(f32[48]{0:T(128)} %copy-done.184) | copy-start | bytes 580
  623.3 85.2 %copy-start.204 = (f32[48]{0:T(128)S(1)}, f32[48]{0:T(128)}, u32[]{:S(2)}) copy-start(f32[48]{0:T(128)} %copy-done.203) | copy-start | bytes 580
  623.3 85.2 %copy-start.207 = (f32[768]{0:T(1024)S(1)}, f32[768]{0:T(1024)}, u32[]{:S(2)}) copy-start(f32[768]{0:T(1024)} %get-tuple-element.1186) | copy-start | bytes 9220
  717.0 241.8 %reduce-scatter.61.cloned.1.call-start = ((), (), s32[]{:S(2)}) async-start(), calls=%async_computation.35 | async-start | bytes 663552
  719.7 351.4 %reduce-scatter.51.cloned.1.call-start = ((), (), s32[]{:S(2)}) async-start(), calls=%async_computation.30 | async-start | bytes 1327104
  720.4 131.4 %copy-start.84 = (bf16[24,768]{1,0:T(8,128)(2,1)}, bf16[24,768]{1,0:T(8,128)(2,1)S(1)}, u32[]{:S(2)}) copy-start(bf16[24,768]{1,0:T(8,128)(2,1)S(1)} %get-tuple-element.1450) | copy-start | bytes 110596
  849.1 106.0 %copy-start.19 = (bf16[12,48,64]{2,1,0:T(8,128)(2,1)}, bf16[12,48,64]{2,1,0:T(8,128)(2,1)S(1)}, u32[]{:S(2)}) copy-start(bf16[12,48,64]{2,1,0:T(8,128)(2,1)S(1)} %get-tuple-element.543) | copy-start | bytes 221188
  851.6 222.1 %reduce-scatter.53.cloned.1.call-start = ((), (), s32[]{:S(2)}) async-start(), calls=%async_computation.31 | async-start | bytes 1327104
  866.5 326.3 %reduce-scatter.67.cloned.1.call-start = ((), (), s32[]{:S(2)}) async-start(), calls=%async_computation.38 | async-start | bytes 331776
  950.6 244.6 %reduce-scatter.69.cloned.1.call-start = ((), (), s32[]{:S(2)}) async-start(), calls=%async_computation.39 | async-start | bytes 331776
  952.6 278.4 %reduce-scatter.65.cloned.1.call-start = ((), (), s32[]{:S(2)}) async-start(), calls=%async_computation.37 | async-start | bytes 663552
  1066.9 167.5 %reduce-scatter.63.cloned.1.call-start = ((), (), s32[]{:S(2)}) async-start(), calls=%async_computation.36 | async-start | bytes 663552
  1070.8 185.1 %reduce-scatter.57.cloned.1.call-start = ((), (), s32[]{:S(2)}) async-start(), calls=%async_computation.33 | async-start | bytes 1327104
  1183.2 78.8 %reduce-scatter.55.cloned.1.call-start = ((), (), s32[]{:S(2)}) async-start(), calls=%async_computation.32 | async-start | bytes 1327104
  1226.5 137.6 %reduce-scatter.71.cloned.1.call-start = ((), (), s32[]{:S(2)}) async-start(), calls=%async_computation.40 | async-start | bytes 1622016
  1255.4 234.0 %all-reduce.4.cloned.1.call-start = ((), (), s32[]{:S(2)}) async-start(), calls=%async_computation.41 | async-start | bytes 196608
  1273.2 330.1 %reduce-scatter.49.cloned.1.call-start = ((), (), s32[]{:S(2)}) async-start(), calls=%async_computation.29 | async-start | bytes 4866048 | tf_op jit(solution)/shard_map/reduce_scatter | solution.py:434
  1277.4 451.2 %reduce-scatter.43.cloned.1.call-start = ((), (), s32[]{:S(2)}) async-start(), calls=%async_computation.26 | async-start | bytes 7299072 | tf_op jit(solution)/shard_map/reduce_scatter | solution.py:431
  1283.4 613.8 %reduce-scatter.47.cloned.1.call-start = ((), (), s32[]{:S(2)}) async-start(), calls=%async_computation.28 | async-start | bytes 14598144 | tf_op jit(solution)/shard_map/reduce_scatter | solution.py:433
  1296.1 826.6 %reduce-scatter.41.cloned.1.call-start = ((), (), s32[]{:S(2)}) async-start(), calls=%async_computation.25 | async-start | bytes 21897216 | tf_op jit(solution)/shard_map/reduce_scatter | solution.py:430
  1315.2 1288.5 %reduce-scatter.45.cloned.1.call-start = ((), (), s32[]{:S(2)}) async-start(), calls=%async_computation.27 | async-start | bytes 58392576 | tf_op jit(solution)/shard_map/reduce_scatter | solution.py:432
  (222 other events, 1111.9 us)
Sparse Core Ops, SparseCore 0:
  10.9 90.8 all-gather.11
  104.7 56.5 all-gather.27
  164.2 61.3 all-gather.17
  227.8 23.4 all-gather.13
  253.7 23.9 all-gather.15
  280.5 169.6 all-gather.19
  453.1 70.6 all-gather.21
  582.5 22.6 all-gather.23
  621.5 22.7 all-gather.25
  717.1 33.0 reduce-scatter.58
  753.3 34.5 reduce-scatter.60
  851.7 35.5 reduce-scatter.50
  891.4 36.8 reduce-scatter.52
  950.7 31.4 reduce-scatter.66
  985.1 32.9 reduce-scatter.68
  1067.0 32.8 reduce-scatter.64
  1102.8 34.4 reduce-scatter.62
  1183.3 35.1 reduce-scatter.56
  1226.6 35.2 reduce-scatter.54
  1267.0 97.0 reduce-scatter.70
  1369.7 119.5 all-reduce.3
  1495.4 107.8 reduce-scatter.48
  1610.4 118.0 reduce-scatter.42
  1735.0 162.1 reduce-scatter.46
  1904.2 218.5 reduce-scatter.40
  2130.7 472.8 reduce-scatter.44
where the time goes:
time: 2640 us; the launch traced here: 2610 us
  waiting for transfers between devices  1450 us (55%)
  matrix products  668 us (25%)
  blocking collectives  225 us (9%)
  local copies, waits for them, and re-layouts  200 us (8%)
  other arithmetic  48.2 us (2%)
    reduce_scatter x1, waiting for transfers between devices, per_device(): lax.psum_scatter(g_mlp, ('dp', 'seq'), scatter_dimension=0, tiled=True)  481 us
    dot_general x146, matrix products, outer(): lax.dot_general(left_side, right_side, (((0,), (0,)), ((), ())), preferre...  250 us
    dot_general x206, matrix products, linear_t(): lax.dot_general(left_side, right_side, (((1,), (1,)), ((), ())), preferre...  250 us
    reduce_scatter x1, waiting for transfers between devices, per_device(): lax.psum_scatter(g_attn_in, ('dp', 'seq'), scatter_dimension=0, tiled=True)  226 us
    dot_general x146, matrix products, linear(): return jnp.dot(left_side, right_side, preferred_element_type=jnp.float32)  169 us
    reduce_scatter x1, waiting for transfers between devices, per_device(): lax.psum_scatter(g_cross_in, ('dp', 'seq'), scatter_dimension=0, tiled=True)  169 us
    all_gather x1, waiting for transfers between devices, per_device(): lax.all_gather(mlp_w, ('dp', 'seq'), axis=0, tiled=True)  135 us
    reduce_scatter x1, waiting for transfers between devices, per_device(): lax.psum_scatter(g_attn_out, ('dp', 'seq'), scatter_dimension=0, tiled=True)  125 us
  transfers between devices with their start and end apart: 26, of which 14 were waited for; matrix products, arithmetic and copies ran while one was open for 33% of the time, Pallas kernels for 0%

commit v1 on v0

v1 whole, which is shorter than its diff:
```python
import math

import jax
import jax.numpy as jnp
from jax import lax
from jax.experimental import pallas as pl
from jax.experimental.pallas import tpu as pltpu
from jax.sharding import Mesh, PartitionSpec as P

D = 768
HEADS = 12
HD = 64
VIEWS = 3
EPS = 1e-06
NEG = -1e30
SCALE = HD**-0.5
BF = jnp.bfloat16
F32 = jnp.float32


def mm(a, b):
    return lax.dot_general(a, b, (((1,), (0,)), ((), ())), preferred_element_type=F32)


def mm_nt(a, b):
    return lax.dot_general(a, b, (((1,), (1,)), ((), ())), preferred_element_type=F32)


def mm_tn(a, b):
    return lax.dot_general(a, b, (((0,), (0,)), ((), ())), preferred_element_type=F32)


def unit_rows(u):
    centre = jnp.mean(u, axis=-1, keepdims=True)
    spread = u - centre
    rs = lax.rsqrt(jnp.mean(spread * spread, axis=-1, keepdims=True) + EPS)
    return spread * rs, rs


def unit_back(z, rs, dz):
    return rs * (
        dz - jnp.mean(dz, axis=-1, keepdims=True) - z * jnp.mean(dz * z, axis=-1, keepdims=True)
    )


def gelu_parts(u):
    phi = 0.5 * lax.erfc(u * (-(0.5**0.5)))
    return phi


def gelu_slope(u):
    return gelu_parts(u) + u * jnp.exp(-0.5 * u * u) * (1.0 / math.sqrt(2.0 * math.pi))


def rounds_of(moves):
    rounds = []
    for move in moves:
        for group in rounds:
            if all(move[0] != other[0] and move[1] != other[1] for other in group):
                group.append(move)
                break
        else:
            rounds.append([move])
    return rounds


def attend_kernel(heads, parts, idq_ref, idk_ref, q_ref, *rest):
    kv_refs, (o_ref, lse_ref) = rest[: 2 * parts], rest[2 * parts :]
    tq = q_ref.shape[0] * q_ref.shape[2]
    wide = q_ref.shape[3]
    q = q_ref[...].reshape(tq, wide)
    ks = [r[...].reshape(-1, wide) for r in kv_refs[:parts]]
    vs = [r[...].reshape(-1, wide) for r in kv_refs[parts:]]
    k = jnp.concatenate(ks, axis=0)
    v = jnp.concatenate(vs, axis=0)
    allowed = idk_ref[0] == idq_ref[0]
    outs = []
    for n in range(heads):
        cols = slice(n * HD, (n + 1) * HD)
        s = jnp.where(allowed, mm_nt(k[:, cols], q[:, cols]) * SCALE, NEG)
        top = jnp.max(s, axis=0, keepdims=True)
        p = jnp.exp(s - top)
        total = jnp.sum(p, axis=0, keepdims=True)
        lse_ref[0, n : n + 1, :] = top + jnp.log(total)
        pb = (p * (1.0 / total)).astype(BF)
        outs.append(mm(v[:, cols].T, pb).T)
    o_ref[...] = jnp.concatenate(outs, axis=1).astype(BF).reshape(o_ref.shape)


def back_kernel(heads, parts, fused, idq_ref, idk_ref, q_ref, do_ref, *rest):
    if fused:
        kv_refs, outs_refs = rest[: 2 * parts], rest[2 * parts :]
        o_ref, dq_ref = outs_refs[:2]
        dkv_refs = outs_refs[2:]
    else:
        lse_ref = rest[0]
        kv_refs, outs_refs = rest[1 : 1 + 2 * parts], rest[1 + 2 * parts :]
        dq_ref = outs_refs[0]
        dkv_refs = outs_refs[1:]
    tq = q_ref.shape[0] * q_ref.shape[2]
    wide = q_ref.shape[3]
    q = q_ref[...].reshape(tq, wide)
    do = do_ref[...].reshape(tq, wide)
    k = jnp.concatenate([r[...].reshape(-1, wide) for r in kv_refs[:parts]], axis=0)
    v = jnp.concatenate([r[...].reshape(-1, wide) for r in kv_refs[parts:]], axis=0)
    tk = k.shape[0] // parts
    allowed = idk_ref[0] == idq_ref[0]
    os, dqs, dks, dvs = [], [], [], []
    for n in range(heads):
        cols = slice(n * HD, (n + 1) * HD)
        qn, kn, vn, gn = q[:, cols], k[:, cols], v[:, cols], do[:, cols]
        s = jnp.where(allowed, mm_nt(kn, qn) * SCALE, NEG)
        if fused:
            top = jnp.max(s, axis=0, keepdims=True)
            e = jnp.exp(s - top)
            p = e * (1.0 / jnp.sum(e, axis=0, keepdims=True))
        else:
            p = jnp.exp(s - lse_ref[0, n : n + 1, :])
        pb = p.astype(BF)
        if fused:
            os.append(mm(vn.T, pb).T)
        dp = mm_nt(vn, gn)
        delta = jnp.sum(p * dp, axis=0, keepdims=True)
        ds = (p * (dp - delta)).astype(BF)
        dqs.append(mm(kn.T, ds).T * SCALE)
        dks.append(mm(ds, qn) * SCALE)
        dvs.append(mm(pb, gn))
    if fused:
        o_ref[...] = jnp.concatenate(os, axis=1).astype(BF).reshape(o_ref.shape)
    dq_ref[...] = jnp.concatenate(dqs, axis=1).astype(BF).reshape(dq_ref.shape)
    dk = jnp.concatenate(dks, axis=1).astype(BF)
    dv = jnp.concatenate(dvs, axis=1).astype(BF)
    for n in range(parts):
        dkv_refs[n][...] = dk[n * tk : (n + 1) * tk].reshape(dkv_refs[n].shape)
        dkv_refs[parts + n][...] = dv[n * tk : (n + 1) * tk].reshape(dkv_refs[parts + n].shape)


def half_spec(a):
    return pl.BlockSpec((a.shape[0], 1) + a.shape[2:], lambda h: (0, h, 0, 0))


def id_spec(a):
    return pl.BlockSpec((1,) + a.shape[1:], lambda h: (h, 0, 0))


def sds(a, dtype=None):
    return jax.ShapeDtypeStruct(a.shape, dtype or a.dtype)


def attention(name, kernel, ins, specs, outs, out_specs, flops, trans):
    nbytes = sum(a.size * a.dtype.itemsize for a in ins)
    return pl.pallas_call(
        kernel,
        grid=(2,),
        in_specs=specs,
        out_specs=out_specs,
        out_shape=outs,
        name=name,
        compiler_params=pltpu.CompilerParams(vmem_limit_bytes=48 * 1024 * 1024),
        cost_estimate=pl.CostEstimate(
            flops=flops, bytes_accessed=2 * nbytes, transcendentals=trans
        ),
    )(*ins)


def attend(heads, idq, idk, q, ks, vs):
    parts = len(ks)
    kernel = lambda *refs: attend_kernel(heads, parts, *refs)
    ins = [idq, idk, q, *ks, *vs]
    specs = [id_spec(idq), id_spec(idk)] + [half_spec(a) for a in ins[2:]]
    lse = jax.ShapeDtypeStruct((2, 8, idq.shape[2]), F32)
    pairs = 2 * heads * idq.shape[2] * idk.shape[1]
    return attention(
        "attend", kernel, ins, specs, [sds(q), lse], [half_spec(q), id_spec(lse)],
        4 * pairs * HD, pairs,
    )


def attend_back(heads, idq, idk, q, do, lse, ks, vs):
    parts = len(ks)
    kernel = lambda *refs: back_kernel(heads, parts, False, *refs)
    ins = [idq, idk, q, do, lse, *ks, *vs]
    specs = [id_spec(idq), id_spec(idk), half_spec(q), half_spec(do), id_spec(lse)]
    specs += [half_spec(a) for a in ins[5:]]
    outs = [sds(q)] + [sds(a) for a in ks] + [sds(a) for a in vs]
    pairs = 2 * heads * idq.shape[2] * idk.shape[1]
    res = attention(
        "attend_back", kernel, ins, specs, outs, [half_spec(a) for a in outs],
        10 * pairs * HD, pairs,
    )
    return res[0], res[1 : 1 + parts], res[1 + parts :]


def attend_both(heads, idq, idk, q, do, ks, vs):
    parts = len(ks)
    kernel = lambda *refs: back_kernel(heads, parts, True, *refs)
    ins = [idq, idk, q, do, *ks, *vs]
    specs = [id_spec(idq), id_spec(idk)] + [half_spec(a) for a in ins[2:]]
    outs = [sds(q), sds(q)] + [sds(a) for a in ks] + [sds(a) for a in vs]
    pairs = 2 * heads * idq.shape[2] * idk.shape[1]
    res = attention(
        "attend_both", kernel, ins, specs, outs, [half_spec(a) for a in outs],
        12 * pairs * HD, pairs,
    )
    return res[0], res[1], res[2 : 2 + parts], res[2 + parts :]


def solution(mesh):
    dp, seq = mesh.shape["dp"], mesh.shape["seq"]
    G = math.gcd(HEADS, seq)
    while G & (G - 1) or (seq // G) & (seq // G - 1):
        G //= 2
    J = seq // G
    heads = HEADS // G
    wide = heads * HD
    nf, nm = dp // 2, dp // 4
    mesh3 = Mesh(mesh.devices.reshape(dp, G, J), ("dp", "g", "j"))
    everyone = ("dp", "g", "j")

    view_of = [0 if d < nf else (1 if d < nf + nm else 2) for d in range(dp)]
    owner = [
        [r // 2 for r in range(dp)],
        [nf + r // 4 for r in range(dp)],
        [nf + nm + r // 4 for r in range(dp)],
    ]
    slot = [[r % 2 for r in range(dp)], [r % 4 for r in range(dp)], [r % 4 for r in range(dp)]]

    def xor(axis, n, size, x):
        return lax.ppermute(x, axis, [(i, i ^ n) for i in range(size)])

    def per_device(
        view_fine, view_mid, view_coarse, grad_fine, grad_mid, grad_coarse, clip_ids,
        attn_in, attn_out, mlp_w, cross_in, cross_out, norm_gains, biases, ffn_bias,
    ):
        tf, tm, tc = view_fine.shape[1], view_mid.shape[1], view_coarse.shape[1]
        U = 2 * tf
        ff = mlp_w.shape[1]
        cells = clip_ids.shape[1]
        d, g, j = lax.axis_index("dp"), lax.axis_index("g"), lax.axis_index("j")
        v = jnp.where(d < nf, 0, jnp.where(d < nf + nm, 1, 2))
        p = jnp.where(d < nf, 0, 1)

        def table(values, index=d):
            out = jnp.int32(values[-1])
            for i in range(len(values) - 1):
                out = jnp.where(index == i, jnp.int32(values[i]), out)
            return out

        def pick(tag, options, dtype=None):
            out = jnp.zeros_like(options[0])
            for k, option in enumerate(options):
                out = jnp.where(tag == k, option, out)
            return out

        def rows_at(x, start, size):
            return lax.dynamic_slice_in_dim(x, start, size, axis=0)

        sizes = (tf, tm, tc)
        moves = [
            (r, owner[w][r], (w, r))
            for w in range(VIEWS)
            for r in range(dp)
            if r != owner[w][r]
        ]
        view_rounds = rounds_of(moves)

        def grow(x, rows):
            if x.shape[0] == rows:
                return x
            return jnp.concatenate([x, jnp.zeros((rows - x.shape[0], x.shape[1]), x.dtype)], axis=0)

        def to_views(fine, mid, coarse):
            mid_p, coarse_p = grow(mid, tf), grow(coarse, tf)
            got = []
            for group in view_rounds:
                n = max(sizes[w] for _, _, (w, _) in group)
                kind = [3] * dp
                for src, _, (w, _) in group:
                    kind[src] = w
                load = pick(table(kind), [fine[:n], mid_p[:n], coarse_p[:n]])
                got.append(grow(lax.ppermute(load, "dp", [(s, t) for s, t, _ in group]), tf))
            local = pick(v, [fine, mid_p, coarse_p])
            rows = []
            for k in range(4):
                tag = [len(got) + 1] * dp
                for i, group in enumerate(view_rounds):
                    for _, dst, (w, r) in group:
                        if slot[w][r] == k:
                            tag[dst] = i + 1
                for r in range(dp):
                    if owner[view_of[r]][r] == r and slot[view_of[r]][r] == k:
                        tag[r] = 0
                rows.append(pick(table(tag), [local] + got))
            as_fine = jnp.concatenate(rows[:2], axis=0)
            as_mid = jnp.concatenate([x[:tm] for x in rows], axis=0)
            pad = jnp.zeros((tf - 2 * tc, fine.shape[1]), fine.dtype)
            as_coarse = jnp.concatenate(
                [rows[0][:tc], rows[1][:tc], pad, rows[2][:tc], rows[3][:tc], pad], axis=0
            )
            return pick(v, [as_fine, as_mid, as_coarse])

        def place(w, k):
            return (tf * k, tm * k, tf * (k // 2) + tc * (k % 2))[w]

        def from_views(x):
            padded = grow(x, U + tf)
            got = []
            for group in view_rounds:
                n = max(sizes[w] for _, _, (w, _) in group)
                start = [0] * dp
                for _, src, (w, r) in group:
                    start[src] = place(w, slot[w][r])
                load = rows_at(padded, table(start), n)
                got.append(grow(lax.ppermute(load, "dp", [(t, s) for s, t, _ in group]), tf))
            local_start = [0] * dp
            for r in range(dp):
                w = view_of[r]
                if owner[w][r] == r:
                    local_start[r] = place(w, slot[w][r])
            local = rows_at(padded, table(local_start), tf)
            outs = []
            for w in range(VIEWS):
                tag = [0] * dp
                for i, group in enumerate(view_rounds):
                    for _, dst, (w2, r) in group:
                        if w2 == w:
                            tag[r] = i + 1
                outs.append(pick(table(tag), [local] + got)[: sizes[w]])
            return outs

        def half_moves(src_of):
            return [(src, dst, h) for dst, (src, h) in src_of.items()]

        q_src = {}
        k_src = {}
        for dst in range(dp):
            if dst < nf:
                q_src[dst] = (nf + (2 * dst) // 4, dst % 2)
            else:
                i = dst - nf
                q_src[dst] = (nf + nm + (2 * i) // 4, i % 2)
                k_src[dst] = (nf + (2 * i) // 4, i % 2)

        def to_cross(x, src_of):
            groups = rounds_of([m for m in half_moves(src_of) if m[0] != m[1]])
            got = []
            for group in groups:
                start = [0] * dp
                for src, _, h in group:
                    start[src] = h * tf
                got.append(
                    lax.ppermute(
                        rows_at(x, table(start), tf), "dp", [(s, t) for s, t, _ in group]
                    )
                )
            start = [0] * dp
            tag = [len(got) + 1] * dp
            for dst, (src, h) in src_of.items():
                if src == dst:
                    start[dst], tag[dst] = h * tf, 0
            for i, group in enumerate(groups):
                for _, dst, _ in group:
                    tag[dst] = i + 1
            return pick(table(tag), [rows_at(x, table(start), tf)] + got)

        def from_cross(x, src_of):
            groups = rounds_of([m for m in half_moves(src_of) if m[0] != m[1]])
            got = [
                lax.ppermute(x, "dp", [(t, s) for s, t, _ in group]) for group in groups
            ]
            halves = []
            for half in range(2):
                tag = [len(got) + 1] * dp
                for dst, (src, h) in src_of.items():
                    if h == half:
                        if src == dst:
                            tag[src] = 0
                        else:
                            for i, group in enumerate(groups):
                                if any(m[1] == dst for m in group):
                                    tag[src] = i + 1
                halves.append(pick(table(tag), [x] + got))
            return jnp.concatenate(halves, axis=0)

        def zeros(rows, like):
            return jnp.zeros((rows, like.shape[1]), like.dtype)

        def q_spread(x):
            z = zeros(tm - tc, x)
            return jnp.where(
                p == 0, x, jnp.concatenate([x[:tc], z, x[tc : 2 * tc], z], axis=0)
            )

        def q_gather(x):
            z = zeros(tf - 2 * tc, x)
            return jnp.where(
                p == 0, x, jnp.concatenate([x[:tc], x[tm : tm + tc], z], axis=0)
            )

        def k_spread(x):
            z = zeros(tf - tm, x)
            return jnp.concatenate([x[:tm], z, x[tm : 2 * tm], z], axis=0)

        def k_gather(x):
            return jnp.concatenate([x[:tm], x[tf : tf + tm]], axis=0)

        def spread_g(x):
            return [x] + [xor("g", m, G, x) for m in range(1, G)]

        def sum_g(pieces):
            out = pieces[0].astype(F32)
            got = [xor("g", m, G, pieces[m].astype(BF)) for m in range(1, G)]
            for x in got:
                out = out + x.astype(F32)
            return out

        def spread_j(x):
            return [x] + [xor("j", n, J, x) for n in range(1, J)]

        n_dev = dp * seq
        vec = jnp.concatenate(
            [
                norm_gains.reshape(-1), biases.reshape(-1), ffn_bias.reshape(-1),
                clip_ids.astype(BF).reshape(-1),
            ]
        )
        vec = jnp.broadcast_to(vec[None], (n_dev, vec.shape[0]))
        vecs = lax.all_to_all(vec, everyone, 0, 0, tiled=True)
        gw, bw, fw = norm_gains.shape[1], biases.shape[1], ffn_bias.shape[1]

        def unpack(start, rows, width):
            part = vecs[:, start : start + rows * width].astype(F32)
            return part.reshape(n_dev, rows, width).transpose(1, 0, 2).reshape(rows, n_dev * width)

        gains = unpack(0, 10, gw)
        vectors = unpack(10 * gw, 28, bw)
        ffn_rows = unpack(10 * gw + 28 * bw, 3, fw)
        ids_at = 10 * gw + 28 * bw + 3 * fw
        ids_all = vecs.reshape(dp, seq, -1)[:, 0, ids_at : ids_at + cells].astype(F32)

        enc_gain = pick(v, [gains[2 * i : 2 * i + 2] for i in range(3)])
        enc_bias = pick(v, [vectors[6 * i : 6 * i + 6] for i in range(3)])
        g1, g2 = enc_gain[0], enc_gain[1]
        n1, bq, bv, bo, n2, bm = [enc_bias[i] for i in range(6)]
        bf_row = pick(v, [ffn_rows[i] for i in range(3)])
        gq = pick(v, [gains[6], gains[6], gains[8]])
        gk = pick(v, [gains[7], gains[9], gains[9]])
        nq = pick(v, [vectors[18], vectors[18], vectors[23]])
        nk = pick(v, [vectors[19], vectors[24], vectors[24]])
        cq, cv, co = [jnp.where(p == 0, vectors[20 + i], vectors[25 + i]) for i in range(3)]

        def cols(x, width):
            return lax.dynamic_slice_in_dim(x, g * width, width, axis=-1)

        before = jnp.stack(
            [jnp.sum((ids_all < c).astype(F32), axis=1) for c in (1, 2, 3)], axis=1
        ).astype(jnp.int32)
        before = jnp.concatenate([before, jnp.zeros((4, 3), jnp.int32)], axis=0)
        s_grid = (
            (g ^ jnp.arange(G, dtype=jnp.int32))[None, :, None] * J
            + (j ^ jnp.arange(J, dtype=jnp.int32))[:, None, None]
        )

        def id_of(cell, starts):
            return sum((cell >= starts[..., c]).astype(jnp.int32) for c in range(3))

        u = jnp.arange(tf, dtype=jnp.int32)[None, None, :]
        base = table([2 * x if x < nf else 4 * ((x - nf) % nm) for x in range(dp)])
        view_starts = rows_at(before, base, 4)

        def view_ids(h):
            is_fine, is_mid = v == 0, v == 1
            unit = jnp.where(is_fine, tf, jnp.where(is_mid, tm, tc))
            second = (u >= unit) & ~is_fine
            first_row = jnp.where(is_fine, h, 2 * h)
            a = rows_at(view_starts, first_row, 1)[0]
            b = rows_at(view_starts, 2 * h + 1, 1)[0]
            starts = jnp.where(second[..., None], b, a)
            pos = s_grid * unit + u - jnp.where(second, unit, 0)
            cell = pos // jnp.where(is_fine, 4, jnp.where(is_mid, 2, 1))
            ids = id_of(cell, starts) + jnp.where(second, 4, 0)
            return jnp.where((u >= 2 * unit) & ~is_fine, -1, ids)

        def cross_ids(h, unit0, unit1, div0, div1, length):
            w = u[..., :length]
            a = rows_at(before, 2 * jnp.where(p == 0, d, d - nf) + h, 1)[0]
            unit = jnp.where(p == 0, unit0, unit1)
            cell = (s_grid * unit + w) // jnp.where(p == 0, div0, div1)
            return jnp.where(w >= unit, -1, id_of(cell, a))

        def as_q(ids):
            return jnp.stack([x[0].reshape(1, -1) for x in ids])

        def as_k(ids):
            return jnp.stack([x.reshape(-1, 1) for x in ids])

        self_ids = [view_ids(h) for h in range(2)]
        idq, idk = as_q(self_ids), as_k(self_ids)
        cross_idq = as_q([cross_ids(h, tm, tc, 2, 1, tm) for h in range(2)])
        cross_idk = as_k([cross_ids(h, tf, tm, 4, 2, tf) for h in range(2)])

        near = dp == 4

        def both_sides(x):
            up = lax.ppermute(x, "dp", [(0, 1), (1, 2), (2, 3)])
            down = lax.ppermute(x, "dp", [(1, 0), (3, 2)])
            return up, down

        def chunks(x):
            if near:
                up, down = both_sides(x)
                enc = jnp.stack([jnp.where(d == 0, x, up), jnp.where(d == 0, down, x)])
                odd = d % 2 == 1
                cross = jnp.stack([jnp.where(odd, up, x), jnp.where(odd, x, down)])
                return enc, cross
            everything = lax.all_gather(x, "dp", axis=0)
            return everything, everything

        enc_lo = jnp.maximum(d - 1, 0) if near else jnp.int32(0)
        cross_lo = 2 * p if near else jnp.int32(0)

        def start_of(part, n_parts, low, total):
            return part * (total // n_parts) - low * (total // dp)

        def join_j(x):
            xs = spread_j(x)
            parts = []
            for a in range(J):
                out = xs[0]
                for n in range(1, J):
                    out = jnp.where((j ^ n) == a, xs[n], out)
                parts.append(out)
            full = jnp.stack(parts, axis=2)
            return full.reshape(-1, x.shape[-1])

        r_in, r_cross = attn_in.shape[0], cross_in.shape[0]
        qkv = lax.all_to_all(
            jnp.concatenate([attn_in, cross_in], axis=0), "g", 1, 0, tiled=True
        ).reshape(G, r_in + r_cross, wide)
        hid = ff // G
        mlp = lax.all_to_all(mlp_w, "g", 1, 0, tiled=True).reshape(G, mlp_w.shape[0], hid)

        enc_c, cross_c = chunks(qkv)
        w_in = rows_at(
            join_j(enc_c[:, :, :r_in]), start_of(v, 3, enc_lo, n_dev * r_in), 3 * D
        )
        c_in = rows_at(
            join_j(cross_c[:, :, r_in:]), start_of(p, 2, cross_lo, n_dev * r_cross), 3 * D
        )
        enc_c, _ = chunks(mlp)
        w_mlp = rows_at(
            join_j(enc_c), start_of(v, 3, enc_lo, n_dev * mlp_w.shape[0]), 2 * D
        )
        r_out, r_co = attn_out.shape[0], cross_out.shape[0]
        enc_c, cross_c = chunks(jnp.concatenate([attn_out, cross_out], axis=0))
        planes = enc_c.shape[0]
        outs = jnp.concatenate([enc_c[:, :r_out], cross_c[:, r_out:]], axis=1)
        outs = lax.all_gather(outs.reshape(-1, D), ("g", "j"), axis=0)
        outs = outs.reshape(seq, planes, r_out + r_co, D).transpose(1, 0, 2, 3)
        w_out = rows_at(
            outs[:, :, :r_out].reshape(-1, D), start_of(v, 3, enc_lo, n_dev * r_out), D
        )
        c_out = rows_at(
            outs[:, :, r_out:].reshape(-1, D), start_of(p, 2, cross_lo, n_dev * r_co), D
        )

        def by_head_group(w):
            return jnp.concatenate([rows_at(w, (g ^ m) * wide, wide) for m in range(G)], axis=0)

        w_out, c_out = by_head_group(w_out), by_head_group(c_out)
        wq, wk, wv = w_in[:D], w_in[D : 2 * D], w_in[2 * D :]
        ccq, cck, ccv = c_in[:D], c_in[D : 2 * D], c_in[2 * D :]
        w1, w2 = w_mlp[:D], w_mlp[D:]

        x_own = to_views(view_fine[0], view_mid[0], view_coarse[0])
        grad_own = to_views(grad_fine[0], grad_mid[0], grad_coarse[0])
        x = jnp.concatenate(spread_g(x_own), axis=0).astype(F32)
        a = (unit_rows(x)[0] * g1 + n1).astype(BF)
        q = (mm(a, wq) + cols(bq, wide)).astype(BF)
        k = mm(a, wk).astype(BF)
        w = (mm(a, wv) + cols(bv, wide)).astype(BF)

        def halves(t, width=None):
            return t.reshape(G, 2, -1, t.shape[-1])

        kv = spread_j(jnp.concatenate([k, w], axis=1))
        ks = [halves(t[:, :wide]) for t in kv]
        vs = [halves(t[:, wide:]) for t in kv]
        o, lse = attend(heads, idq, idk, halves(q), ks, vs)

        def all_heads(t):
            t = t.reshape(G, -1, wide)
            got = [t]
            for m in range(1, G):
                r = xor("g", m, G, t)
                got.append(jnp.stack([r[i ^ m] for i in range(G)]))
            return jnp.concatenate(got, axis=2).reshape(-1, G * wide)

        o_all = all_heads(o)
        h = x + (mm(o_all, w_out) + bo)
        zh, _ = unit_rows(h)
        c = (zh * g2 + n2).astype(BF)
        up = mm(c, w1) + cols(bf_row, hid)
        e = (up * gelu_parts(up)).astype(BF)
        y_part = mm_nt(e, w2).reshape(G, U, D)
        h_own = h[:U]
        y = sum_g([y_part[m] for m in range(G)]) + h_own + bm

        zy, rs_y = unit_rows(y)
        kn_v = (zy * gk + nk).astype(BF)
        qn_v = (zy * gq + nq).astype(BF)
        kn_own = jnp.where(p == 0, kn_v, k_spread(to_cross(kn_v, k_src)))
        qn_own = q_spread(to_cross(qn_v, q_src))
        gq_own = q_spread(to_cross(grad_own, q_src))
        kn = jnp.concatenate(spread_g(kn_own), axis=0)
        qn = jnp.concatenate(spread_g(qn_own), axis=0)
        gc = jnp.concatenate(spread_g(gq_own), axis=0)
        cross_q = (mm(qn, ccq) + cols(cq, wide)).astype(BF)
        cross_k = mm(kn, cck).astype(BF)
        cross_v = (mm(kn, ccv) + cols(cv, wide)).astype(BF)
        d_att = mm_nt(gc, c_out[:wide]).astype(BF)
        kv = spread_j(jnp.concatenate([cross_k, cross_v], axis=1))
        cks = [halves(t[:, :wide]) for t in kv]
        cvs = [halves(t[:, wide:]) for t in kv]
        co_att, dq_c, dks, dvs = attend_both(
            heads, cross_idq, cross_idk, halves(cross_q), halves(d_att), cks, cvs
        )

        def home_j(ts):
            out = ts[0].astype(F32)
            for n in range(1, J):
                out = out + xor("j", n, J, ts[n]).astype(F32)
            return out

        def home_kv(dks, dvs):
            both = home_j([jnp.concatenate([a, b], axis=3) for a, b in zip(dks, dvs)])
            both = both.astype(BF).reshape(-1, 2 * wide)
            return both[:, :wide], both[:, wide:]

        dk_c, dv_c = home_kv(dks, dvs)
        dq_c = dq_c.reshape(-1, wide)
        cross_o = all_heads(co_att)
        Uq = 2 * tm
        mix = mm(cross_o[:Uq], c_out) + co
        mix_v = from_cross(q_gather(mix.astype(BF)), q_src).astype(F32)

        dqn_part = mm_nt(dq_c, ccq).reshape(G, Uq, D)
        dqn = sum_g([dqn_part[m] for m in range(G)]).astype(BF)
        dkn_part = (mm_nt(dk_c, cck) + mm_nt(dv_c, ccv)).reshape(G, U, D)
        dkn = sum_g([dkn_part[m] for m in range(G)]).astype(BF)
        dqn_v = from_cross(q_gather(dqn), q_src).astype(F32)
        dkn_v = jnp.where(v == 0, dkn, from_cross(k_gather(dkn), k_src)).astype(F32)
        dqn_v = jnp.where(v == 0, 0.0, dqn_v)
        mix_v = jnp.where(v == 0, 0.0, mix_v)
        dkn_v = jnp.where(v == 2, 0.0, dkn_v)
        dy = grad_own.astype(F32) + unit_back(zy, rs_y, dqn_v * gq + dkn_v * gk)

        dm_own = dy.astype(BF)
        dm = jnp.concatenate(spread_g(dm_own), axis=0)
        de = mm(dm, w2)
        du = (de * gelu_slope(up)).astype(BF)
        dc_part = mm_nt(du, w1).reshape(G, U, D)
        dn2 = sum_g([dc_part[m] for m in range(G)])
        zh_own, rs_h = unit_rows(h_own)
        dh = dy + unit_back(zh_own, rs_h, dn2 * g2)
        dh_own = dh.astype(BF)
        dh_all = jnp.concatenate(spread_g(dh_own), axis=0)
        d_o = mm_nt(dh_all, w_out[:wide]).astype(BF)
        dq, dks, dvs = attend_back(heads, idq, idk, halves(q), halves(d_o), lse, ks, vs)
        dk, dv = home_kv(dks, dvs)
        dq = dq.reshape(-1, wide)
        da_part = (mm_nt(dq, wq) + mm_nt(dk, wk) + mm_nt(dv, wv)).reshape(G, U, D)
        da = sum_g([da_part[m] for m in range(G)])
        zx, rs_x = unit_rows(x_own.astype(F32))
        dx = dh + unit_back(zx, rs_x, da * g1)

        out_f, out_m, out_c = from_views((y + mix_v).astype(BF))
        dx_f, dx_m, dx_c = from_views(dx.astype(BF))

        def my_rows(x):
            return lax.dynamic_index_in_dim(x, j, axis=2, keepdims=False)

        def send_home(grad, total, enc):
            width = grad.shape[1]
            r = total // n_dev
            if near:
                frame_rows, n_planes = total // 2, 2
                low = enc_lo if enc else cross_lo
            else:
                frame_rows, n_planes, low = total, dp, jnp.int32(0)
            if grad.shape[0] != frame_rows:
                part, n_parts = (v, 3) if enc else (p, 2)
                grad = lax.dynamic_update_slice_in_dim(
                    jnp.zeros((frame_rows, width), BF), grad.astype(BF),
                    start_of(part, n_parts, low, total), axis=0,
                )
            x = grad.astype(BF).reshape(n_planes, G, J, r, width)
            acc = lax.dynamic_index_in_dim(x, j, axis=2, keepdims=False).astype(F32)
            for n in range(1, J):
                part = lax.dynamic_index_in_dim(x, j ^ n, axis=2, keepdims=False)
                acc = acc + xor("j", n, J, part).astype(F32)
            if not near:
                acc = lax.psum_scatter(acc, "dp", scatter_dimension=0, tiled=False)
            elif enc:
                own = jnp.where(d == 0, acc[0], acc[1])
                other = jnp.where(d == 0, acc[1], acc[0]).astype(BF)
                down = lax.ppermute(other, "dp", [(1, 0), (2, 1), (3, 2)])
                upward = lax.ppermute(other, "dp", [(0, 1)])
                acc = own + down.astype(F32) + upward.astype(F32)
            else:
                odd = d % 2 == 1
                own = jnp.where(odd, acc[1], acc[0])
                other = jnp.where(odd, acc[0], acc[1]).astype(BF)
                acc = own + xor("dp", 1, dp, other).astype(F32)
            acc = acc.astype(BF).reshape(G * r, width)
            return lax.all_to_all(acc, "g", 0, 1, tiled=True).astype(F32)

        def in_order(w):
            return jnp.concatenate(
                [rows_at(w, (g ^ a) * wide, wide) for a in range(G)], axis=0
            )

        g_cin = jnp.concatenate([mm_tn(qn, dq_c), mm_tn(kn, dk_c), mm_tn(kn, dv_c)], axis=0)
        g_cout = in_order(mm_tn(cross_o, cols(gc, wide)))
        g_mlp = jnp.concatenate([mm_tn(c, du), mm_tn(dm, e)], axis=0)
        g_out = in_order(mm_tn(o_all, cols(dh_all, wide)))
        g_in = jnp.concatenate([mm_tn(a, dq), mm_tn(a, dk), mm_tn(a, dv)], axis=0)
        grad_cin = send_home(g_cin, n_dev * r_cross, False)
        grad_cout = send_home(g_cout, n_dev * r_co, False)
        grad_mlp = send_home(g_mlp, n_dev * mlp_w.shape[0], True)
        grad_out = send_home(g_out, n_dev * r_out, True)
        grad_in = send_home(g_in, n_dev * r_in, True)

        def total(x):
            return jnp.sum(x.astype(F32), axis=0)

        def at_cols(x):
            hot = (jnp.arange(G) == g).astype(F32)
            return (hot[:, None] * x[None]).reshape(-1)

        def at_row(x, index, n):
            hot = (jnp.arange(n) == index).astype(F32)
            return hot.reshape((n,) + (1,) * x.ndim) * x[None]

        enc_g = jnp.stack([total(da * zx), total(dn2 * zh_own)])
        enc_b = jnp.stack(
            [
                total(da), at_cols(total(dq)), at_cols(total(dv)), total(dh_own), total(dn2),
                total(dm_own),
            ]
        )
        q_role = at_row(jnp.stack([total(dqn_v * zy), total(dqn_v), total(grad_own)]), v - 1, 2)
        k_role = at_row(jnp.stack([total(dkn_v * zy), total(dkn_v)]), v, 2)
        pair = at_row(jnp.stack([at_cols(total(dq_c)), at_cols(total(dv_c))]), p, 2)
        gains_g = jnp.concatenate(
            [
                at_row(enc_g, v, 3).reshape(6, D),
                jnp.stack([q_role[:, 0], k_role[:, 0]], axis=1).reshape(4, D),
            ]
        )
        cross_b = jnp.stack(
            [q_role[:, 1], k_role[:, 1], pair[:, 0], pair[:, 1], q_role[:, 2]], axis=1
        )
        bias_g = jnp.concatenate([at_row(enc_b, v, 3).reshape(18, D), cross_b.reshape(10, D)])
        ffn_g = at_row(at_cols(total(du)), v, 3)

        def split(x):
            n = x.shape[0]
            return x.reshape(n, n_dev, -1).transpose(1, 0, 2).reshape(n_dev, -1)

        small = jnp.concatenate([split(gains_g), split(bias_g), split(ffn_g)], axis=1)
        small = jnp.sum(lax.all_to_all(small, everyone, 0, 0, tiled=True), axis=0)
        n_g, n_b = 10 * gw, 28 * bw
        return (
            out_f[None], out_m[None], out_c[None],
            dx_f.astype(F32)[None], dx_m.astype(F32)[None], dx_c.astype(F32)[None],
            grad_in, grad_out, grad_mlp, grad_cin, grad_cout,
            small[:n_g].reshape(10, gw),
            small[n_g : n_g + n_b].reshape(28, bw),
            small[n_g + n_b :].reshape(3, fw),
        )

    tokens = P("dp", ("g", "j"), None)
    rows = P(everyone, None)
    columns = P(None, everyone)
    return jax.shard_map(
        per_device,
        mesh=mesh3,
        in_specs=(tokens,) * 6 + (P("dp", None),) + (rows,) * 5 + (columns,) * 3,
        out_specs=(tokens,) * 6 + (rows,) * 5 + (columns,) * 3,
        check_vma=False,
    )
```

time: 2640 us -> 680 us (0.26)
  waiting for transfers between devices: 1450 us -> 120 us
  matrix products: 668 us -> 61.1 us
  blocking collectives: 225 us -> 0 us
  starting transfers between devices: 2.02 us -> 182 us
  other arithmetic: 48.2 us -> 105 us
  local copies, waits for them, and re-layouts: 200 us -> 159 us
    reduce_scatter x5 -> x0, waiting for transfers between devices: 1110 us -> none  [the longest x1 481 us: per_device(): lax.psum_scatter(g_mlp, ('dp', 'seq'), scatter_dimension=0, tiled=True)]
    dot_general x498 -> x30, matrix products: 668 us -> 61.1 us  [the longest x10 23.9 us: mm(): lax.dot_general(a, b, (((1,), (0,)), ((), ())), preferred_element_type=F32)]
    all_gather x9 -> x1, waiting for transfers between devices: 238 us -> 0.01 us  [per_device(): outs = lax.all_gather(outs.reshape(-1, D), ('g', 'j'), axis=0)]
    all_gather x9 -> x0, blocking collectives: 184 us -> none  [the longest x1 44.4 us: per_device(): lax.all_gather(norm_gains, ('dp', 'seq'), axis=1, tiled=True)]
    ppermute x0 -> x91, starting transfers between devices: none -> 142 us  [the longest x53 55.8 us: xor(): return lax.ppermute(x, axis, [(i, i ^ n) for i in range(size)])]
    ppermute x0 -> x91, waiting for transfers between devices: none -> 109 us  [the longest x53 57.9 us: xor(): return lax.ppermute(x, axis, [(i, i ^ n) for i in range(size)])]
    unnamed x38 -> x1, waiting for transfers between devices: 96.2 us -> 0.02 us
    unnamed x559 -> x390, local copies, waits for them, and re-layouts: 74.5 us -> 11.8 us
  transfers between devices with their start and end apart: 26 -> 101, of which waited for: 14 -> 30; matrix products, arithmetic and copies ran while one was open for 33% -> 43% of each run, Pallas kernels for 0% -> 2%
where the time goes in v1:
time: 680 us; the launch traced here: 668 us
  starting transfers between devices  182 us (27%)
  local copies, waits for them, and re-layouts  159 us (23%)
  waiting for transfers between devices  120 us (18%)
  other arithmetic  105 us (15%)
  matrix products  61.1 us (9%)
  Pallas kernels  22 us (3%)
  between operations  18.7 us (3%)
    ppermute x53, waiting for transfers between devices, xor(): return lax.ppermute(x, axis, [(i, i ^ n) for i in range(size)])  57.9 us
    ppermute x53, starting transfers between devices, xor(): return lax.ppermute(x, axis, [(i, i ^ n) for i in range(size)])  55.8 us
    dot_general x10, matrix products, mm(): lax.dot_general(a, b, (((1,), (0,)), ((), ())), preferred_element_type=F32)  23.9 us
    ppermute x8, starting transfers between devices, from_views(): lax.ppermute(load, 'dp', [(t, s) for s, t, _ in group])  22.3 us
    pallas_call x3, Pallas kernels, attention(): pl.pallas_call(kernel, grid=(2,), in_specs=specs, out_specs=out_specs, ou...  22 us
    dot_general x10, matrix products, mm_nt(): lax.dot_general(a, b, (((1,), (1,)), ((), ())), preferred_element_type=F32)  21.3 us
    all_to_all x5, starting transfers between devices, send_home(): return lax.all_to_all(acc, 'g', 0, 1, tiled=True).astype(F32)  18.6 us
    ppermute x8, starting transfers between devices, to_views(): lax.ppermute(load, 'dp', [(s, t) for s, t, _ in group])  16.5 us
  transfers between devices with their start and end apart: 101, of which 30 were waited for; matrix products, arithmetic and copies ran while one was open for 43% of the time, Pallas kernels for 2%

profile of v1, /device:TPU:0, one launch (start us, length us, event | category | flops | bytes accessed | tf_op | source)
XLA Modules:
  0.0 668.0 jit_solution(17592588704130359665)
XLA Ops:
  9.2 6.9 %collective-permute-start.2 = (bf16[96,768]{1,0:T(8,128)(2,1)}, bf16[96,768]{1,0:T(8,128)(2,1)S(1)}, u32[]{:S(2)}, u32[]{:S(2)}) collective-permute-start(bf16[96,768]{1,0:T(8,128)(2,1)} %get-tuple-element.258), channel_id=1, source_target_pairs={{24,8},{8,16},{0,24},{25,9},{9,17},{1,25},{26,10},{10,18},{2,26},{... | collective-permute-start | bytes 442376 | tf_op jit(solution)/shard_map/ppermute | solution.py:281
  28.3 7.8 %all-to-all-start = ((bf16[32,2,696]{2,1,0:T(2,128)(2,1)}), bf16[32,2,696]{2,1,0:T(2,128)(2,1)S(1)}, u32[]{:S(2)}, u32[]{:S(2)}) async-start(bf16[32,2,696]{2,1,0:T(2,128)(2,1)} %reshape.1546), calls=%async_computation | async-start | bytes 196608 | tf_op jit(solution)/shard_map/all_to_all | solution.py:428
  37.3 4.4 collective-permute-start.14
  57.0 2.5 collective-permute-start.30
  72.6 4.3 all-to-all-start.1
  138.9 4.5 add_select_fusion.9
  151.7 4.1 add_select_fusion.3
  161.1 12.4 %collective-permute-done.33 = bf16[96,768]{1,0:T(8,128)(2,1)} collective-permute-done((bf16[96,768]{1,0:T(8,128)(2,1)S(1)}, bf16[96,768]{1,0:T(8,128)(2,1)}, u32[]{:S(2)}, u32[]{:S(2)}) %collective-permute-start.33) | collective-permute-done | bytes 147488 | tf_op jit(solution)/shard_map/ppermute | solution.py:352
  174.5 4.2 all-to-all-start.2
  182.3 9.0 %collective-permute-done.7 = bf16[4,360,192]{1,2,0:T(8,128)(2,1)S(1)} collective-permute-done((bf16[4,360,192]{1,2,0:T(8,128)(2,1)}, bf16[4,360,192]{1,2,0:T(8,128)(2,1)S(1)}, u32[]{:S(2)}, u32[]{:S(2)}) %collective-permute-start.7) | collective-permute-done | bytes 552992 | tf_op jit(solution)/shard_map/ppermute | solution.py:505
  191.3 4.0 collective-permute-done.8
  202.7 2.6 collective-permute-start.16
  210.9 2.8 copy.375
  213.6 5.3 reshape.1483
  223.8 5.1 collective-permute-done.17
  240.8 5.3 attend.1
  252.3 5.6 collective-permute-done.12
  257.9 2.9 collective-permute-done.11
  262.1 6.1 collective-permute-done.13
  279.8 7.7 %multiply_convert_fusion = (bf16[768,768]{1,0:T(8,128)(2,1)S(1)}, f32[768,768]{1,0:T(8,128)}, f32[768,768]{1,0:T(8,128)}) fusion(f32[768]{0:T(1024)S(1)} %copy-done.158, bf16[2304,768]{1,0:T(8,128)(2,1)S(1)} %bitcast.349, s32[]{:T(128)S(6)} %select_n.1856, f32[768,768]{1,0:T(8,128)S(1)} %get-tuple-element.334, f32[768]{0:T(1024)S(1)} %copy-done.154, ...), kind=kOutput, calls=%fused_computation.24 | convolution fusion | flops 947257344 | bytes 9457668 | tf_op jit(solution)/shard_map/dot_general | solution.py:22
  293.5 5.2 collective-permute-done.19
  298.7 6.1 collective-permute-done.20
  313.1 2.7 collective-permute-done.23
  321.0 6.8 %collective-permute-done.39 = bf16[192,768]{1,0:T(8,128)(2,1)S(1)} collective-permute-done((bf16[192,768]{1,0:T(8,128)(2,1)S(1)}, bf16[192,768]{1,0:T(8,128)(2,1)S(1)}, u32[]{:S(2)}, u32[]{:S(2)}) %collective-permute-start.39) | collective-permute-done | bytes 294944 | tf_op jit(solution)/shard_map/ppermute | solution.py:229
  330.1 3.3 collective-permute-start.26
  345.7 9.8 %attend_both.1 = (bf16[4,2,48,192]{3,2,1,0:T(8,128)(2,1)S(1)}, bf16[4,2,48,192]{3,2,1,0:T(8,128)(2,1)S(1)}, bf16[4,2,96,192]{3,2,1,0:T(8,128)(2,1)S(1)}, bf16[4,...) custom-call(s32[2,1,192]{2,1,0:T(1,128)S(1)} %pad_add_fusion.2.refs_0_, ...), custom_call_target="tpu_custom_call" | custom-call | flops 679477248 | bytes 2964480 | tf_op jit(solution)/shard_map/attend_both/pallas_call | solution.py:152
  371.1 3.0 collective-permute-done.52
  377.5 6.1 collective-permute-start.46
  384.3 3.6 collective-permute-start.55
  388.0 5.2 collective-permute-start.90
  396.5 3.3 all-to-all-start.7
  401.5 3.2 all-to-all-done.7
  417.8 3.6 collective-permute-done.58
  432.5 10.8 %collective-permute-start.50 = (bf16[96,768]{1,0:T(8,128)(2,1)S(1)}, bf16[96,768]{1,0:T(8,128)(2,1)S(1)}, u32[]{:S(2)}, u32[]{:S(2)}) collective-permute-start(bf16[96,768]{1,0:T(8,128)(2,1)S(1)} %get-tuple-element.249), channel_id=1, source_target_pairs={{0,8},{8,16},{16,0},{1,9},{9,17},{17,1},{2,10},{10,18},{18,2},{3,1... | collective-permute-start | bytes 442376 | tf_op jit(solution)/shard_map/ppermute | solution.py:314
  448.4 3.7 collective-permute-start.88
  454.2 2.6 collective-permute-done.88
  457.6 4.1 all-to-all-start.6
  461.8 4.4 convert_reduce_fusion.1
  466.3 3.9 fusion.256
  470.2 2.6 convolution_convert_fusion.1
  477.2 2.8 convolution_convert_fusion
  484.5 2.8 dynamic-slice_bitcast_fusion
  500.3 7.3 %collective-permute-done.68 = bf16[192,768]{1,0:T(8,128)(2,1)S(1)} collective-permute-done((bf16[192,768]{1,0:T(8,128)(2,1)S(1)}, bf16[192,768]{1,0:T(8,128)(2,1)S(1)}, u32[]{:S(2)}, u32[]{:S(2)}) %collective-permute-start.68) | collective-permute-done | bytes 294944 | tf_op jit(solution)/shard_map/ppermute | solution.py:229
  508.3 2.8 fusion.98
  513.9 7.0 %attend_back.1 = (bf16[4,2,96,192]{3,2,1,0:T(8,128)(2,1)S(1)}, bf16[4,2,96,192]{3,2,1,0:T(8,128)(2,1)S(1)}, bf16[4,2,96,192]{3,2,1,0:T(8,128)(2,1)S(1)}, bf16[4,...) custom-call(s32[2,1,384]{2,1,0:T(1,128)S(1)} %constant_dynamic-update-slice_fusion.refs_0_, ...), custom_call_target="tpu_custom_call" | custom-call | flops 1132462080 | bytes 3606528 | tf_op jit(solution)/shard_map/attend_back/pallas_call | solution.py:152
  520.9 3.4 fusion.132
  528.0 4.6 collective-permute-start.83
  536.7 3.5 all-to-all-start.4
  540.3 4.9 all-to-all-done.4
  547.8 2.9 fusion.104
  553.4 4.6 fusion.257
  563.1 6.9 %dynamic_update_slice.9 = bf16[3456,192]{0,1:T(8,128)(2,1)S(1)} dynamic-update-slice(bf16[3456,192]{0,1:T(8,128)(2,1)S(1)} %broadcast_in_dim.238, bf16[2304,192]{0,1:T(8,128)(2,1)S(1)} %pad_maximum_fusion.9, s32[]{:T(128)S(6)} %select_n.1831, s32[]{:T(128)} %constant.231.clone.1) | dynamic-update-slice | bytes 1769476 | tf_op jit(solution)/shard_map/dynamic_update_slice | solution.py:693
  570.0 4.8 reshape.1508
  574.8 4.0 constant_dynamic-slice_fusion
  585.0 5.1 all-to-all-start.8
  590.4 2.5 convert_add_fusion
  595.3 5.5 collective-permute-start.86
  604.1 4.6 collective-permute-start.80
  612.0 14.4 %collective-permute-done.79 = bf16[4,216,192]{1,0,2:T(4,128)(2,1)S(1)} collective-permute-done((bf16[4,216,192]{1,0,2:T(4,128)(2,1)S(1)}, bf16[4,216,192]{1,0,2:T(4,128)(2,1)S(1)}, u32[]{:S(2)}, u32[]{:S(2)}) %collective-permute-start.79) | collective-permute-done | bytes 331808 | tf_op jit(solution)/shard_map/ppermute | solution.py:707
  626.5 5.0 collective-permute-start.77
  635.2 4.1 all-to-all-start.3
  639.3 2.7 fusion.21
  642.0 3.2 all-to-all-done.3
  645.3 3.5 all-to-all-start.5
  (965 shorter events, 334.8 us)
Async XLA Ops:
  9.2 52.9 %collective-permute-start.2 = (bf16[96,768]{1,0:T(8,128)(2,1)}, bf16[96,768]{1,0:T(8,128)(2,1)S(1)}, u32[]{:S(2)}, u32[]{:S(2)}) collective-permute-start(bf16[96,768]{1,0:T(8,128)(2,1)} %get-tuple-element.258), channel_id=1, source_target_pairs={{24,8},{8,16},{0,24},{25,9},{9,17},{1,25},{26,10},{10,18},{2,26},{... | collective-permute-start | bytes 442376 | tf_op jit(solution)/shard_map/ppermute | solution.py:281
  16.1 46.6 %collective-permute-start.3 = (bf16[96,768]{1,0:T(8,128)(2,1)}, bf16[96,768]{1,0:T(8,128)(2,1)S(1)}, u32[]{:S(2)}, u32[]{:S(2)}) collective-permute-start(bf16[96,768]{1,0:T(8,128)(2,1)} %get-tuple-element.257), channel_id=1, source_target_pairs={{8,0},{16,8},{0,16},{9,1},{17,9},{1,17},{10,2},{18,10},{2,18},{11,... | collective-permute-start | bytes 442376 | tf_op jit(solution)/shard_map/ppermute | solution.py:281
  19.7 39.8 %collective-permute-start.1 = (bf16[48,768]{1,0:T(8,128)(2,1)}, bf16[48,768]{1,0:T(8,128)(2,1)S(1)}, u32[]{:S(2)}, u32[]{:S(2)}) collective-permute-start(bf16[48,768]{1,0:T(8,128)(2,1)} %fusion.166), channel_id=1, source_target_pairs={{24,16},{8,24},{25,17},{9,25},{26,18},{10,26},{27,19},{11,27},{28,... | collective-permute-start | bytes 221192 | tf_op jit(solution)/shard_map/ppermute | solution.py:281
  21.8 35.2 %collective-permute-start = (bf16[24,768]{1,0:T(8,128)(2,1)}, bf16[24,768]{1,0:T(8,128)(2,1)S(1)}, u32[]{:S(2)}, u32[]{:S(2)}) collective-permute-start(bf16[24,768]{1,0:T(8,128)(2,1)} %bitcast_select_fusion.4), channel_id=1, source_target_pairs={{16,24},{17,25},{18,26},{19,27},{20,28},{21,29},{22,30},{23,31}} | collective-permute-start | bytes 110600 | tf_op jit(solution)/shard_map/ppermute | solution.py:281
  28.3 44.4 %all-to-all-start = ((bf16[32,2,696]{2,1,0:T(2,128)(2,1)}), bf16[32,2,696]{2,1,0:T(2,128)(2,1)S(1)}, u32[]{:S(2)}, u32[]{:S(2)}) async-start(bf16[32,2,696]{2,1,0:T(2,128)(2,1)} %reshape.1546), calls=%async_computation | async-start | bytes 196608 | tf_op jit(solution)/shard_map/all_to_all | solution.py:428
  37.3 119.8 %collective-permute-start.14 = (bf16[120,768]{1,0:T(8,128)(2,1)}, bf16[120,768]{1,0:T(8,128)(2,1)}, u32[]{:S(2)}, u32[]{:S(2)}) collective-permute-start(bf16[120,768]{1,0:T(8,128)(2,1)} %constant_dynamic-update-slice_fusion.2), channel_id=1, source_target_pairs={{0,8},{8,16},{16,24},{1,9},{9,17},{17,25},{2,10},{10,18},{18,26},{... | collective-permute-start | bytes 552968 | tf_op jit(solution)/shard_map/ppermute | solution.py:505
  64.2 93.6 %collective-permute-start.15 = (bf16[120,768]{1,0:T(8,128)(2,1)}, bf16[120,768]{1,0:T(8,128)(2,1)}, u32[]{:S(2)}, u32[]{:S(2)}) collective-permute-start(bf16[120,768]{1,0:T(8,128)(2,1)} %constant_dynamic-update-slice_fusion.2), channel_id=1, source_target_pairs={{8,0},{24,16},{9,1},{25,17},{10,2},{26,18},{11,3},{27,19},{12,4},{... | collective-permute-start | bytes 552968 | tf_op jit(solution)/shard_map/ppermute | solution.py:506
  65.5 116.5 %collective-permute-start.4 = (bf16[192,768]{1,0:T(8,128)(2,1)S(1)}, bf16[192,768]{1,0:T(8,128)(2,1)S(1)}, u32[]{:S(2)}, u32[]{:S(2)}) collective-permute-start(bf16[192,768]{1,0:T(8,128)(2,1)S(1)} %get-tuple-element.140), channel_id=1, source_target_pairs={{0,2},{2,0},{4,6},{6,4},{1,3},{3,1},{5,7},{7,5},{8,10},{10,8},{12,... | collective-permute-start | bytes 884744 | tf_op jit(solution)/shard_map/ppermute | solution.py:229
  67.1 114.9 %collective-permute-start.5 = (bf16[192,768]{1,0:T(8,128)(2,1)S(1)}, bf16[192,768]{1,0:T(8,128)(2,1)S(1)}, u32[]{:S(2)}, u32[]{:S(2)}) collective-permute-start(bf16[192,768]{1,0:T(8,128)(2,1)S(1)} %get-tuple-element.140), channel_id=1, source_target_pairs={{0,4},{2,6},{4,0},{6,2},{1,5},{3,7},{5,1},{7,3},{8,12},{10,14},{12... | collective-permute-start | bytes 884744 | tf_op jit(solution)/shard_map/ppermute | solution.py:229
  68.6 113.4 %collective-permute-start.6 = (bf16[192,768]{1,0:T(8,128)(2,1)S(1)}, bf16[192,768]{1,0:T(8,128)(2,1)S(1)}, u32[]{:S(2)}, u32[]{:S(2)}) collective-permute-start(bf16[192,768]{1,0:T(8,128)(2,1)S(1)} %get-tuple-element.140), channel_id=1, source_target_pairs={{0,6},{2,4},{4,2},{6,0},{1,7},{3,5},{5,3},{7,1},{8,14},{10,12},{12... | collective-permute-start | bytes 884744 | tf_op jit(solution)/shard_map/ppermute | solution.py:229
  72.6 101.9 %all-to-all-start.1 = ((bf16[360,4,192]{0,2,1:T(8,128)(2,1)}), bf16[360,4,192]{0,2,1:T(8,128)(2,1)}, u32[]{:S(2)}, u32[]{:S(2)}) async-start(bf16[360,4,192]{0,2,1:T(8,128)(2,1)} %bitcast.22), calls=%async_computation.1 | async-start | bytes 1179648 | tf_op jit(solution)/shard_map/all_to_all | solution.py:537
  76.9 195.4 %all-gather.2.cloned.1.call-start = ((), (), s32[]{:S(2)}) async-start(), calls=%async_computation.9 | async-start | bytes 3317760 | tf_op jit(solution)/shard_map/all_gather | solution.py:558
  157.8 15.7 %collective-permute-start.33 = (bf16[96,768]{1,0:T(8,128)(2,1)S(1)}, bf16[96,768]{1,0:T(8,128)(2,1)}, u32[]{:S(2)}, u32[]{:S(2)}) collective-permute-start(bf16[96,768]{1,0:T(8,128)(2,1)S(1)} %copy-done.106), channel_id=1, source_target_pairs={{16,0},{24,16},{17,1},{25,17},{18,2},{26,18},{19,3},{27,19},{20,4}... | collective-permute-start | bytes 442376 | tf_op jit(solution)/shard_map/ppermute | solution.py:352
  174.5 28.2 %all-to-all-start.2 = ((bf16[144,4,768]{2,0,1:T(8,128)(2,1)}), bf16[144,4,768]{2,0,1:T(8,128)(2,1)}, u32[]{:S(2)}, u32[]{:S(2)}) async-start(bf16[144,4,768]{2,0,1:T(8,128)(2,1)} %bitcast.298), calls=%async_computation.2 | async-start | bytes 1769472 | tf_op jit(solution)/shard_map/all_to_all | solution.py:541
  178.7 12.6 %collective-permute-start.7 = (bf16[4,360,192]{1,2,0:T(8,128)(2,1)}, bf16[4,360,192]{1,2,0:T(8,128)(2,1)S(1)}, u32[]{:S(2)}, u32[]{:S(2)}) collective-permute-start(bf16[4,360,192]{1,2,0:T(8,128)(2,1)} %bitcast.23), channel_id=1, source_target_pairs={{0,8},{8,16},{16,24},{1,9},{9,17},{17,25},{2,10},{10,18},{18,26},{... | collective-permute-start | bytes 1658888 | tf_op jit(solution)/shard_map/ppermute | solution.py:505
  180.0 15.3 %collective-permute-start.8 = (bf16[4,360,192]{1,2,0:T(8,128)(2,1)}, bf16[4,360,192]{1,2,0:T(8,128)(2,1)S(1)}, u32[]{:S(2)}, u32[]{:S(2)}) collective-permute-start(bf16[4,360,192]{1,2,0:T(8,128)(2,1)} %bitcast.23), channel_id=1, source_target_pairs={{8,0},{24,16},{9,1},{25,17},{10,2},{26,18},{11,3},{27,19},{12,4},{... | collective-permute-start | bytes 1658888 | tf_op jit(solution)/shard_map/ppermute | solution.py:506
  202.7 21.1 %collective-permute-start.16 = (bf16[4,144,768]{2,1,0:T(8,128)(2,1)}, bf16[4,144,768]{2,1,0:T(8,128)(2,1)}, u32[]{:S(2)}, u32[]{:S(2)}) collective-permute-start(bf16[4,144,768]{2,1,0:T(8,128)(2,1)} %bitcast.48), channel_id=1, source_target_pairs={{0,8},{8,16},{16,24},{1,9},{9,17},{17,25},{2,10},{10,18},{18,26},{... | collective-permute-start | bytes 2654216 | tf_op jit(solution)/shard_map/ppermute | solution.py:505
  205.4 23.5 %collective-permute-start.17 = (bf16[4,144,768]{2,1,0:T(8,128)(2,1)}, bf16[4,144,768]{2,1,0:T(8,128)(2,1)}, u32[]{:S(2)}, u32[]{:S(2)}) collective-permute-start(bf16[4,144,768]{2,1,0:T(8,128)(2,1)} %bitcast.48), channel_id=1, source_target_pairs={{8,0},{24,16},{9,1},{25,17},{10,2},{26,18},{11,3},{27,19},{12,4},{... | collective-permute-start | bytes 2654216 | tf_op jit(solution)/shard_map/ppermute | solution.py:506
  223.0 14.3 %collective-permute-start.10 = (bf16[768,384]{0,1:T(8,128)(2,1)}, bf16[768,384]{0,1:T(8,128)(2,1)}, u32[]{:S(2)}, u32[]{:S(2)}) collective-permute-start(bf16[768,384]{0,1:T(8,128)(2,1)} %pad_maximum_fusion.14), channel_id=1, source_target_pairs={{0,1},{1,0},{2,3},{3,2},{4,5},{5,4},{6,7},{7,6},{8,9},{9,8},{10,11... | collective-permute-start | bytes 1769480 | tf_op jit(solution)/shard_map/ppermute | solution.py:229
  232.3 36.1 %collective-permute-start.18 = (bf16[2,4,144,768]{3,2,1,0:T(8,128)(2,1)}, bf16[2,4,144,768]{3,2,1,0:T(8,128)(2,1)}, u32[]{:S(2)}, u32[]{:S(2)}) collective-permute-start(bf16[2,4,144,768]{3,2,1,0:T(8,128)(2,1)} %pad_maximum_fusion.1), channel_id=1, source_target_pairs={{0,1},{1,0},{2,3},{3,2},{4,5},{5,4},{6,7},{7,6},{8,9},{9,8},{10,11... | collective-permute-start | bytes 5308424 | tf_op jit(solution)/shard_map/ppermute | solution.py:229
  246.1 11.8 %collective-permute-start.12 = (bf16[4,192,192]{2,1,0:T(8,128)(2,1)}, bf16[4,192,192]{2,1,0:T(8,128)(2,1)S(1)}, u32[]{:S(2)}, u32[]{:S(2)}) collective-permute-start(bf16[4,192,192]{2,1,0:T(8,128)(2,1)} %bitcast.36), channel_id=1, source_target_pairs={{0,4},{2,6},{4,0},{6,2},{1,5},{3,7},{5,1},{7,3},{8,12},{10,14},{12... | collective-permute-start | bytes 884744 | tf_op jit(solution)/shard_map/ppermute | solution.py:229
  248.5 12.3 %collective-permute-start.11 = (bf16[4,192,192]{2,1,0:T(8,128)(2,1)}, bf16[4,192,192]{2,1,0:T(8,128)(2,1)}, u32[]{:S(2)}, u32[]{:S(2)}) collective-permute-start(bf16[4,192,192]{2,1,0:T(8,128)(2,1)} %bitcast.36), channel_id=1, source_target_pairs={{0,2},{2,0},{4,6},{6,4},{1,3},{3,1},{5,7},{7,5},{8,10},{10,8},{12,... | collective-permute-start | bytes 884744 | tf_op jit(solution)/shard_map/ppermute | solution.py:229
  252.0 16.2 %collective-permute-start.13 = (bf16[4,192,192]{2,1,0:T(8,128)(2,1)}, bf16[4,192,192]{2,1,0:T(8,128)(2,1)S(1)}, u32[]{:S(2)}, u32[]{:S(2)}) collective-permute-start(bf16[4,192,192]{2,1,0:T(8,128)(2,1)} %bitcast.36), channel_id=1, source_target_pairs={{0,6},{2,4},{4,2},{6,0},{1,7},{3,5},{5,3},{7,1},{8,14},{10,12},{12... | collective-permute-start | bytes 884744 | tf_op jit(solution)/shard_map/ppermute | solution.py:229
  290.5 14.4 %collective-permute-start.20 = (bf16[192,768]{1,0:T(8,128)(2,1)S(1)}, bf16[192,768]{1,0:T(8,128)(2,1)S(1)}, u32[]{:S(2)}, u32[]{:S(2)}) collective-permute-start(bf16[192,768]{1,0:T(8,128)(2,1)S(1)} %get-tuple-element.187), channel_id=1, source_target_pairs={{0,4},{2,6},{4,0},{6,2},{1,5},{3,7},{5,1},{7,3},{8,12},{10,14},{12... | collective-permute-start | bytes 884744 | tf_op jit(solution)/shard_map/ppermute | solution.py:229
  291.9 12.9 %collective-permute-start.21 = (bf16[192,768]{1,0:T(8,128)(2,1)S(1)}, bf16[192,768]{1,0:T(8,128)(2,1)S(1)}, u32[]{:S(2)}, u32[]{:S(2)}) collective-permute-start(bf16[192,768]{1,0:T(8,128)(2,1)S(1)} %get-tuple-element.186), channel_id=1, source_target_pairs={{0,6},{2,4},{4,2},{6,0},{1,7},{3,5},{5,3},{7,1},{8,14},{10,12},{12... | collective-permute-start | bytes 884744 | tf_op jit(solution)/shard_map/ppermute | solution.py:229
  310.8 17.0 %collective-permute-start.39 = (bf16[192,768]{1,0:T(8,128)(2,1)S(1)}, bf16[192,768]{1,0:T(8,128)(2,1)S(1)}, u32[]{:S(2)}, u32[]{:S(2)}) collective-permute-start(bf16[192,768]{1,0:T(8,128)(2,1)S(1)} %maximum_select_fusion.4), channel_id=1, source_target_pairs={{0,4},{2,6},{4,0},{6,2},{1,5},{3,7},{5,1},{7,3},{8,12},{10,14},{12... | collective-permute-start | bytes 884744 | tf_op jit(solution)/shard_map/ppermute | solution.py:229
  311.6 16.2 %collective-permute-start.40 = (bf16[192,768]{1,0:T(8,128)(2,1)S(1)}, bf16[192,768]{1,0:T(8,128)(2,1)S(1)}, u32[]{:S(2)}, u32[]{:S(2)}) collective-permute-start(bf16[192,768]{1,0:T(8,128)(2,1)S(1)} %maximum_select_fusion.4), channel_id=1, source_target_pairs={{0,6},{2,4},{4,2},{6,0},{1,7},{3,5},{5,3},{7,1},{8,14},{10,12},{12... | collective-permute-start | bytes 884744 | tf_op jit(solution)/shard_map/ppermute | solution.py:229
  316.7 13.3 %collective-permute-start.34 = (bf16[96,768]{1,0:T(8,128)(2,1)S(1)}, bf16[96,768]{1,0:T(8,128)(2,1)S(1)}, u32[]{:S(2)}, u32[]{:S(2)}) collective-permute-start(bf16[96,768]{1,0:T(8,128)(2,1)S(1)} %get-tuple-element.295), channel_id=1, source_target_pairs={{0,2},{2,0},{4,6},{6,4},{1,3},{3,1},{5,7},{7,5},{8,10},{10,8},{12,... | collective-permute-start | bytes 442376 | tf_op jit(solution)/shard_map/ppermute | solution.py:229
  318.0 15.7 %collective-permute-start.35 = (bf16[96,768]{1,0:T(8,128)(2,1)S(1)}, bf16[96,768]{1,0:T(8,128)(2,1)S(1)}, u32[]{:S(2)}, u32[]{:S(2)}) collective-permute-start(bf16[96,768]{1,0:T(8,128)(2,1)S(1)} %get-tuple-element.295), channel_id=1, source_target_pairs={{0,4},{2,6},{4,0},{6,2},{1,5},{3,7},{5,1},{7,3},{8,12},{10,14},{12... | collective-permute-start | bytes 442376 | tf_op jit(solution)/shard_map/ppermute | solution.py:229
  319.6 14.1 %collective-permute-start.36 = (bf16[96,768]{1,0:T(8,128)(2,1)S(1)}, bf16[96,768]{1,0:T(8,128)(2,1)S(1)}, u32[]{:S(2)}, u32[]{:S(2)}) collective-permute-start(bf16[96,768]{1,0:T(8,128)(2,1)S(1)} %get-tuple-element.295), channel_id=1, source_target_pairs={{0,6},{2,4},{4,2},{6,0},{1,7},{3,5},{5,3},{7,1},{8,14},{10,12},{12... | collective-permute-start | bytes 442376 | tf_op jit(solution)/shard_map/ppermute | solution.py:229
  355.5 12.2 %collective-permute-start.42 = (bf16[4,96,192]{2,1,0:T(8,128)(2,1)S(1)}, bf16[4,96,192]{2,1,0:T(8,128)(2,1)S(1)}, u32[]{:S(2)}, u32[]{:S(2)}) collective-permute-start(bf16[4,96,192]{2,1,0:T(8,128)(2,1)S(1)} %bitcast.322), channel_id=1, source_target_pairs={{0,2},{2,0},{4,6},{6,4},{1,3},{3,1},{5,7},{7,5},{8,10},{10,8},{12,... | collective-permute-start | bytes 442376 | tf_op jit(solution)/shard_map/ppermute | solution.py:229
  358.4 12.2 %collective-permute-start.43 = (bf16[4,96,192]{2,1,0:T(8,128)(2,1)S(1)}, bf16[4,96,192]{2,1,0:T(8,128)(2,1)S(1)}, u32[]{:S(2)}, u32[]{:S(2)}) collective-permute-start(bf16[4,96,192]{2,1,0:T(8,128)(2,1)S(1)} %bitcast.324), channel_id=1, source_target_pairs={{0,4},{2,6},{4,0},{6,2},{1,5},{3,7},{5,1},{7,3},{8,12},{10,14},{12... | collective-permute-start | bytes 442376 | tf_op jit(solution)/shard_map/ppermute | solution.py:229
  367.9 37.8 %collective-permute-start.56 = (bf16[4,2,96,384]{3,2,1,0:T(8,128)(2,1)}, bf16[4,2,96,384]{3,2,1,0:T(8,128)(2,1)}, u32[]{:S(2)}, u32[]{:S(2)}) collective-permute-start(bf16[4,2,96,384]{3,2,1,0:T(8,128)(2,1)} %pad_maximum_fusion.18), channel_id=1, source_target_pairs={{0,1},{1,0},{2,3},{3,2},{4,5},{5,4},{6,7},{7,6},{8,9},{9,8},{10,11... | collective-permute-start | bytes 1769480 | tf_op jit(solution)/shard_map/ppermute | solution.py:229
  376.8 11.3 %collective-permute-start.45 = (bf16[96,768]{1,0:T(8,128)(2,1)S(1)}, bf16[96,768]{1,0:T(8,128)(2,1)S(1)}, u32[]{:S(2)}, u32[]{:S(2)}) collective-permute-start(bf16[96,768]{1,0:T(8,128)(2,1)S(1)} %get-tuple-element.288), channel_id=1, source_target_pairs={{8,16},{9,17},{10,18},{11,19},{12,20},{13,21},{14,22},{15,23}} | collective-permute-start | bytes 442376 | tf_op jit(solution)/shard_map/ppermute | solution.py:369
  377.5 15.8 %collective-permute-start.46 = (bf16[96,768]{1,0:T(8,128)(2,1)S(1)}, bf16[96,768]{1,0:T(8,128)(2,1)S(1)}, u32[]{:S(2)}, u32[]{:S(2)}) collective-permute-start(bf16[96,768]{1,0:T(8,128)(2,1)S(1)} %get-tuple-element.288), channel_id=1, source_target_pairs={{0,16},{16,24},{1,17},{17,25},{2,18},{18,26},{3,19},{19,27},{4,20}... | collective-permute-start | bytes 442376 | tf_op jit(solution)/shard_map/ppermute | solution.py:369
  383.6 16.2 %collective-permute-start.54 = (bf16[96,768]{1,0:T(8,128)(2,1)S(1)}, bf16[96,768]{1,0:T(8,128)(2,1)S(1)}, u32[]{:S(2)}, u32[]{:S(2)}) collective-permute-start(bf16[96,768]{1,0:T(8,128)(2,1)S(1)} %get-tuple-element.287), channel_id=1, source_target_pairs={{8,16},{9,17},{10,18},{11,19},{12,20},{13,21},{14,22},{15,23}} | collective-permute-start | bytes 442376 | tf_op jit(solution)/shard_map/ppermute | solution.py:369
  384.3 15.5 %collective-permute-start.55 = (bf16[96,768]{1,0:T(8,128)(2,1)S(1)}, bf16[96,768]{1,0:T(8,128)(2,1)}, u32[]{:S(2)}, u32[]{:S(2)}) collective-permute-start(bf16[96,768]{1,0:T(8,128)(2,1)S(1)} %get-tuple-element.287), channel_id=1, source_target_pairs={{0,16},{16,24},{1,17},{17,25},{2,18},{18,26},{3,19},{19,27},{4,20}... | collective-permute-start | bytes 442376 | tf_op jit(solution)/shard_map/ppermute | solution.py:369
  424.8 19.3 %collective-permute-start.87 = (bf16[2,4,144,192]{3,2,1,0:T(8,128)(2,1)}, bf16[2,4,144,192]{3,2,1,0:T(8,128)(2,1)}, u32[]{:S(2)}, u32[]{:S(2)}) collective-permute-start(bf16[2,4,144,192]{3,2,1,0:T(8,128)(2,1)} %dynamic-slice_bitcast_fusion.1), channel_id=1, source_target_pairs={{0,1},{1,0},{2,3},{3,2},{4,5},{5,4},{6,7},{7,6},{8,9},{9,8},{10,11... | collective-permute-start | bytes 1327112 | tf_op jit(solution)/shard_map/ppermute | solution.py:229
  427.7 34.1 %collective-permute-start.61 = (bf16[192,768]{1,0:T(8,128)(2,1)S(1)}, bf16[192,768]{1,0:T(8,128)(2,1)}, u32[]{:S(2)}, u32[]{:S(2)}) collective-permute-start(bf16[192,768]{1,0:T(8,128)(2,1)S(1)} %get-tuple-element.131), channel_id=1, source_target_pairs={{0,2},{2,0},{4,6},{6,4},{1,3},{3,1},{5,7},{7,5},{8,10},{10,8},{12,... | collective-permute-start | bytes 884744 | tf_op jit(solution)/shard_map/ppermute | solution.py:229
  431.2 17.2 %collective-permute-start.49 = (bf16[96,768]{1,0:T(8,128)(2,1)S(1)}, bf16[96,768]{1,0:T(8,128)(2,1)S(1)}, u32[]{:S(2)}, u32[]{:S(2)}) collective-permute-start(bf16[96,768]{1,0:T(8,128)(2,1)S(1)} %get-tuple-element.250), channel_id=1, source_target_pairs={{8,24},{16,8},{24,0},{9,25},{17,9},{25,1},{10,26},{18,10},{26,2},{... | collective-permute-start | bytes 442376 | tf_op jit(solution)/shard_map/ppermute | solution.py:314
  432.5 19.6 %collective-permute-start.50 = (bf16[96,768]{1,0:T(8,128)(2,1)S(1)}, bf16[96,768]{1,0:T(8,128)(2,1)S(1)}, u32[]{:S(2)}, u32[]{:S(2)}) collective-permute-start(bf16[96,768]{1,0:T(8,128)(2,1)S(1)} %get-tuple-element.249), channel_id=1, source_target_pairs={{0,8},{8,16},{16,0},{1,9},{9,17},{17,1},{2,10},{10,18},{18,2},{3,1... | collective-permute-start | bytes 442376 | tf_op jit(solution)/shard_map/ppermute | solution.py:314
  446.0 15.7 %collective-permute-start.62 = (bf16[192,768]{1,0:T(8,128)(2,1)S(1)}, bf16[192,768]{1,0:T(8,128)(2,1)S(1)}, u32[]{:S(2)}, u32[]{:S(2)}) collective-permute-start(bf16[192,768]{1,0:T(8,128)(2,1)S(1)} %get-tuple-element.131), channel_id=1, source_target_pairs={{0,4},{2,6},{4,0},{6,2},{1,5},{3,7},{5,1},{7,3},{8,12},{10,14},{12... | collective-permute-start | bytes 884744 | tf_op jit(solution)/shard_map/ppermute | solution.py:229
  446.9 14.8 %collective-permute-start.63 = (bf16[192,768]{1,0:T(8,128)(2,1)S(1)}, bf16[192,768]{1,0:T(8,128)(2,1)S(1)}, u32[]{:S(2)}, u32[]{:S(2)}) collective-permute-start(bf16[192,768]{1,0:T(8,128)(2,1)S(1)} %get-tuple-element.131), channel_id=1, source_target_pairs={{0,6},{2,4},{4,2},{6,0},{1,7},{3,5},{5,3},{7,1},{8,14},{10,12},{12... | collective-permute-start | bytes 884744 | tf_op jit(solution)/shard_map/ppermute | solution.py:229
  457.6 37.0 %all-to-all-start.6 = ((bf16[4,144,192]{2,1,0:T(8,128)(2,1)}), bf16[4,144,192]{2,1,0:T(8,128)(2,1)}, u32[]{:S(2)}, u32[]{:S(2)}) async-start(bf16[4,144,192]{2,1,0:T(8,128)(2,1)} %fusion.94), calls=%async_computation.6 | async-start | bytes 589824 | tf_op jit(solution)/shard_map/all_to_all | solution.py:716
  473.7 13.6 %collective-permute-start.64 = (bf16[192,768]{1,0:T(8,128)(2,1)}, bf16[192,768]{1,0:T(8,128)(2,1)}, u32[]{:S(2)}, u32[]{:S(2)}) collective-permute-start(bf16[192,768]{1,0:T(8,128)(2,1)} %get-tuple-element.171), channel_id=1, source_target_pairs={{0,2},{2,0},{4,6},{6,4},{1,3},{3,1},{5,7},{7,5},{8,10},{10,8},{12,... | collective-permute-start | bytes 884744 | tf_op jit(solution)/shard_map/ppermute | solution.py:229
  475.6 11.9 %collective-permute-start.65 = (bf16[192,768]{1,0:T(8,128)(2,1)}, bf16[192,768]{1,0:T(8,128)(2,1)}, u32[]{:S(2)}, u32[]{:S(2)}) collective-permute-start(bf16[192,768]{1,0:T(8,128)(2,1)} %get-tuple-element.173), channel_id=1, source_target_pairs={{0,4},{2,6},{4,0},{6,2},{1,5},{3,7},{5,1},{7,3},{8,12},{10,14},{12... | collective-permute-start | bytes 884744 | tf_op jit(solution)/shard_map/ppermute | solution.py:229
  487.3 103.2 %collective-permute-start.84 = (bf16[2,4,144,768]{3,2,1,0:T(8,128)(2,1)}, bf16[2,4,144,768]{3,2,1,0:T(8,128)(2,1)}, u32[]{:S(2)}, u32[]{:S(2)}) collective-permute-start(bf16[2,4,144,768]{3,2,1,0:T(8,128)(2,1)} %dynamic-slice_bitcast_fusion), channel_id=1, source_target_pairs={{0,1},{1,0},{2,3},{3,2},{4,5},{5,4},{6,7},{7,6},{8,9},{9,8},{10,11... | collective-permute-start | bytes 5308424 | tf_op jit(solution)/shard_map/ppermute | solution.py:229
  492.2 15.4 %collective-permute-start.68 = (bf16[192,768]{1,0:T(8,128)(2,1)S(1)}, bf16[192,768]{1,0:T(8,128)(2,1)S(1)}, u32[]{:S(2)}, u32[]{:S(2)}) collective-permute-start(bf16[192,768]{1,0:T(8,128)(2,1)S(1)} %get-tuple-element.134), channel_id=1, source_target_pairs={{0,4},{2,6},{4,0},{6,2},{1,5},{3,7},{5,1},{7,3},{8,12},{10,14},{12... | collective-permute-start | bytes 884744 | tf_op jit(solution)/shard_map/ppermute | solution.py:229
  493.7 13.9 %collective-permute-start.69 = (bf16[192,768]{1,0:T(8,128)(2,1)S(1)}, bf16[192,768]{1,0:T(8,128)(2,1)S(1)}, u32[]{:S(2)}, u32[]{:S(2)}) collective-permute-start(bf16[192,768]{1,0:T(8,128)(2,1)S(1)} %get-tuple-element.134), channel_id=1, source_target_pairs={{0,6},{2,4},{4,2},{6,0},{1,7},{3,5},{5,3},{7,1},{8,14},{10,12},{12... | collective-permute-start | bytes 884744 | tf_op jit(solution)/shard_map/ppermute | solution.py:229
  533.6 12.6 %collective-permute-start.70 = (bf16[4,2,96,384]{3,2,1,0:T(8,128)(2,1)}, bf16[4,2,96,384]{3,2,1,0:T(8,128)(2,1)}, u32[]{:S(2)}, u32[]{:S(2)}) collective-permute-start(bf16[4,2,96,384]{3,2,1,0:T(8,128)(2,1)} %pad_maximum_fusion.19), channel_id=1, source_target_pairs={{0,1},{1,0},{2,3},{3,2},{4,5},{5,4},{6,7},{7,6},{8,9},{9,8},{10,11... | collective-permute-start | bytes 1769480 | tf_op jit(solution)/shard_map/ppermute | solution.py:229
  559.0 21.8 %collective-permute-start.71 = (bf16[192,768]{1,0:T(8,128)(2,1)}, bf16[192,768]{1,0:T(8,128)(2,1)S(1)}, u32[]{:S(2)}, u32[]{:S(2)}) collective-permute-start(bf16[192,768]{1,0:T(8,128)(2,1)} %get-tuple-element.168), channel_id=1, source_target_pairs={{0,2},{2,0},{4,6},{6,4},{1,3},{3,1},{5,7},{7,5},{8,10},{10,8},{12,... | collective-permute-start | bytes 884744 | tf_op jit(solution)/shard_map/ppermute | solution.py:229
  560.0 20.9 %collective-permute-start.72 = (bf16[192,768]{1,0:T(8,128)(2,1)}, bf16[192,768]{1,0:T(8,128)(2,1)}, u32[]{:S(2)}, u32[]{:S(2)}) collective-permute-start(bf16[192,768]{1,0:T(8,128)(2,1)} %get-tuple-element.170), channel_id=1, source_target_pairs={{0,4},{2,6},{4,0},{6,2},{1,5},{3,7},{5,1},{7,3},{8,12},{10,14},{12... | collective-permute-start | bytes 884744 | tf_op jit(solution)/shard_map/ppermute | solution.py:229
  560.4 20.5 %collective-permute-start.73 = (bf16[192,768]{1,0:T(8,128)(2,1)}, bf16[192,768]{1,0:T(8,128)(2,1)}, u32[]{:S(2)}, u32[]{:S(2)}) collective-permute-start(bf16[192,768]{1,0:T(8,128)(2,1)} %get-tuple-element.169), channel_id=1, source_target_pairs={{0,6},{2,4},{4,2},{6,0},{1,7},{3,5},{5,3},{7,1},{8,14},{10,12},{12... | collective-permute-start | bytes 884744 | tf_op jit(solution)/shard_map/ppermute | solution.py:229
  580.8 20.0 %collective-permute-start.78 = (bf16[2,4,216,192]{2,1,0,3:T(4,128)(2,1)}, bf16[2,4,216,192]{2,1,0,3:T(4,128)(2,1)}, u32[]{:S(2)}, u32[]{:S(2)}) collective-permute-start(bf16[2,4,216,192]{2,1,0,3:T(4,128)(2,1)} %copy.421), channel_id=1, source_target_pairs={{0,1},{1,0},{2,3},{3,2},{4,5},{5,4},{6,7},{7,6},{8,9},{9,8},{10,11... | collective-permute-start | bytes 1990664 | tf_op jit(solution)/shard_map/ppermute | solution.py:229
  585.0 50.2 %all-to-all-start.8 = ((f32[32,1,1200]{2,1,0:T(1,128)}), f32[32,1,1200]{2,1,0:T(1,128)}, u32[]{:S(2)}, u32[]{:S(2)}) async-start(f32[32,1,1200]{2,1,0:T(1,128)} %copy.437), calls=%async_computation.8 | async-start | bytes 327680 | tf_op jit(solution)/shard_map/all_to_all | solution.py:772
  594.0 39.9 %collective-permute-start.85 = (bf16[4,144,768]{2,1,0:T(8,128)(2,1)}, bf16[4,144,768]{2,1,0:T(8,128)(2,1)}, u32[]{:S(2)}, u32[]{:S(2)}) collective-permute-start(bf16[4,144,768]{2,1,0:T(8,128)(2,1)} %fusion.54), channel_id=1, source_target_pairs={{8,0},{16,8},{24,16},{9,1},{17,9},{25,17},{10,2},{18,10},{26,18},{... | collective-permute-start | bytes 2654216 | tf_op jit(solution)/shard_map/ppermute | solution.py:707
  595.3 44.0 %collective-permute-start.86 = (bf16[4,144,768]{2,1,0:T(8,128)(2,1)}, bf16[4,144,768]{2,1,0:T(8,128)(2,1)}, u32[]{:S(2)}, u32[]{:S(2)}) collective-permute-start(bf16[4,144,768]{2,1,0:T(8,128)(2,1)} %fusion.54), channel_id=1, source_target_pairs={{0,8},{1,9},{2,10},{3,11},{4,12},{5,13},{6,14},{7,15}} | collective-permute-start | bytes 2654216 | tf_op jit(solution)/shard_map/ppermute | solution.py:708
  602.8 23.7 %collective-permute-start.79 = (bf16[4,216,192]{1,0,2:T(4,128)(2,1)S(1)}, bf16[4,216,192]{1,0,2:T(4,128)(2,1)S(1)}, u32[]{:S(2)}, u32[]{:S(2)}) collective-permute-start(bf16[4,216,192]{1,0,2:T(4,128)(2,1)S(1)} %fusion.97), channel_id=1, source_target_pairs={{8,0},{16,8},{24,16},{9,1},{17,9},{25,17},{10,2},{18,10},{26,18},{... | collective-permute-start | bytes 995336 | tf_op jit(solution)/shard_map/ppermute | solution.py:707
  604.1 27.4 %collective-permute-start.80 = (bf16[4,216,192]{1,0,2:T(4,128)(2,1)S(1)}, bf16[4,216,192]{1,0,2:T(4,128)(2,1)S(1)}, u32[]{:S(2)}, u32[]{:S(2)}) collective-permute-start(bf16[4,216,192]{1,0,2:T(4,128)(2,1)S(1)} %fusion.97), channel_id=1, source_target_pairs={{0,8},{1,9},{2,10},{3,11},{4,12},{5,13},{6,14},{7,15}} | collective-permute-start | bytes 995336 | tf_op jit(solution)/shard_map/ppermute | solution.py:708
  610.7 38.1 %collective-permute-start.76 = (bf16[96,768]{1,0:T(8,128)(2,1)}, bf16[96,768]{1,0:T(8,128)(2,1)}, u32[]{:S(2)}, u32[]{:S(2)}) collective-permute-start(bf16[96,768]{1,0:T(8,128)(2,1)} %get-tuple-element.244), channel_id=1, source_target_pairs={{8,24},{16,8},{24,0},{9,25},{17,9},{25,1},{10,26},{18,10},{26,2},{... | collective-permute-start | bytes 442376 | tf_op jit(solution)/shard_map/ppermute | solution.py:314
  626.5 22.4 %collective-permute-start.77 = (bf16[96,768]{1,0:T(8,128)(2,1)}, bf16[96,768]{1,0:T(8,128)(2,1)}, u32[]{:S(2)}, u32[]{:S(2)}) collective-permute-start(bf16[96,768]{1,0:T(8,128)(2,1)} %get-tuple-element.243), channel_id=1, source_target_pairs={{0,8},{8,16},{16,0},{1,9},{9,17},{17,1},{2,10},{10,18},{18,2},{3,1... | collective-permute-start | bytes 442376 | tf_op jit(solution)/shard_map/ppermute | solution.py:314
  631.5 17.3 %collective-permute-start.75 = (bf16[48,768]{1,0:T(8,128)(2,1)}, bf16[48,768]{1,0:T(8,128)(2,1)}, u32[]{:S(2)}, u32[]{:S(2)}) collective-permute-start(bf16[48,768]{1,0:T(8,128)(2,1)} %pad_dynamic-slice_fusion.5), channel_id=1, source_target_pairs={{16,24},{24,8},{17,25},{25,9},{18,26},{26,10},{19,27},{27,11},{20,... | collective-permute-start | bytes 221192 | tf_op jit(solution)/shard_map/ppermute | solution.py:314
  633.9 14.9 %collective-permute-start.74 = (bf16[24,768]{1,0:T(8,128)(2,1)}, bf16[24,768]{1,0:T(8,128)(2,1)}, u32[]{:S(2)}, u32[]{:S(2)}) collective-permute-start(bf16[24,768]{1,0:T(8,128)(2,1)} %pad_dynamic-slice_fusion.6), channel_id=1, source_target_pairs={{24,16},{25,17},{26,18},{27,19},{28,20},{29,21},{30,22},{31,23}} | collective-permute-start | bytes 110600 | tf_op jit(solution)/shard_map/ppermute | solution.py:314
  645.3 13.9 %all-to-all-start.5 = ((bf16[4,144,768]{2,1,0:T(8,128)(2,1)}), bf16[4,144,768]{2,1,0:T(8,128)(2,1)S(1)}, u32[]{:S(2)}, u32[]{:S(2)}) async-start(bf16[4,144,768]{2,1,0:T(8,128)(2,1)} %fusion.21), calls=%async_computation.5 | async-start | bytes 1769472 | tf_op jit(solution)/shard_map/all_to_all | solution.py:716
  (222 other events, 1959.8 us)
Sparse Core Ops, SparseCore 0:
  161.2 45.9 all-gather.1
